TPU v7x, 128 devices: a whole 4x4x4 slice. The times are simulated.
128 devices in a mesh: req: 16 (over x, y), head: 8 (over z, core).
Axes of the slice: x: 4, y: 4, z: 4, core: 2. Of those that a mesh axis runs over, the one named last changes fastest.
Arguments:
- streams: bfloat16 [12288, 4, 2048], P('req', None, 'head'), may hold values from -6 to 6
- hc_in: float32 [2, 4], replicated, may hold values from 0.2 to 1
- hc_mix: float32 [2, 4, 4], replicated, may hold values from -0.4 to 0.4
- hc_out: float32 [2, 4], replicated, may hold values from 0.5 to 1.5
- qkv_weight: bfloat16 [2048, 3, 2048], P(None, None, 'head'), may hold values from -0.125 to 0.125
- out_weight: bfloat16 [2048, 2048], P('head'), may hold values from -0.125 to 0.125
- up_gate: bfloat16 [2048, 2, 8192], P(None, None, 'head'), may hold values from -0.125 to 0.125
- down_weight: bfloat16 [8192, 2048], P('head'), may hold values from -0.0625 to 0.0625
- draft_weight: bfloat16 [2, 2048, 2048], P(None, None, 'head'), may hold values from -0.125 to 0.125
- lm_head: bfloat16 [2048, 50304], P(None, ('req', 'head')), may hold values from -0.125 to 0.125
- k_pages: bfloat16 [768, 128, 16, 128], P('req', None, 'head'), may hold values from -45 to 45
- v_pages: bfloat16 [768, 128, 16, 128], P('req', None, 'head'), may hold values from -6 to 6
- page_owner: int32 [768], P('req'), may hold values from -1 to 255, as said below
- page_fill: int32 [768], P('req'), may hold values from 0 to 128, as said below
- cache_len: int32 [256], P('req'), may hold values from 1 to 16384, as said below
- tree_parent: int32 [256, 48], P('req'), may hold values from 0 to 46, as said below
- accepted_index: int32 [256], P('req'), may hold values from 0 to 47
Outputs:
- new_streams: bfloat16 [12288, 4, 2048], P('req', None, 'head')
- logits: float32 [256, 2, 50304], P(('req', 'head'))
Inputs may be any that keep to these rules, and one draw needn't show every extreme that they name: `page_owner`: each page slot holds one page of the request it names, or -1 where it is empty. Every request owns at least one page and one request owns 128 pages; the live pages of a device's slots vary widely from device to device. `page_fill`: 0 for an empty slot; every page of a request is full except at most one. `cache_len`: equals the valid entries of the pages the request owns; one request has exactly 16384. `tree_parent`: entry i names a smaller position, the parent of position i; position 0 is the root and names itself.
All inputs are finite; a program needn't handle non-finite values.
Results may differ from a plain program's by a relative error of at most 0.027.
Values may be sent and summed in bfloat16 or wider, within the bound.
A program may use at most 512 MiB of HBM per device.

v0:
```python
import functools
import math

import jax
import jax.numpy as jnp
from jax import lax
from jax.experimental import pallas as pl
from jax.experimental.pallas import tpu as pltpu
from jax.sharding import PartitionSpec as P

NEG_FILL = -1e30
PRECISE = lax.Precision.HIGHEST


def layer_norm(values):
    center = jnp.mean(values, axis=-1, keepdims=True)
    square = jnp.mean(values * values, axis=-1, keepdims=True)
    return (values - center) * lax.rsqrt(square - center * center + 1e-05)


def normalize(values, sums, squares, width):
    center = sums / width
    return (values - center) * lax.rsqrt(squares / width - center * center + 1e-05)


def ancestors(parents):
    length = parents.shape[1]
    places = jnp.arange(length, dtype=jnp.int32)
    linked = (parents[:, :, None] == places[None, None, :]) | (places[:, None] == places[None, :])[
        None
    ]
    reach = linked.astype(jnp.float32)
    for repeat in range(max(1, (length - 1).bit_length())):
        reach = jnp.minimum(jnp.einsum("jik,jkl->jil", reach, reach, precision=PRECISE), 1.0)
    return reach


def rotate(values, positions):
    half = values.shape[-1] // 2
    freqs = jnp.exp(
        jnp.arange(half, dtype=jnp.float32) * (-2.0 * math.log(10000.0) / values.shape[-1])
    )
    angles = positions.astype(jnp.float32)[:, None] * freqs[None, :]
    cosine = jnp.cos(angles)[:, None, :]
    sine = jnp.sin(angles)[:, None, :]
    first = values[..., :half]
    second = values[..., half:]
    return jnp.concatenate(
        [first * cosine - second * sine, second * cosine + first * sine], axis=-1
    )


def blend(stream_vals, weights):
    total = weights[0] * stream_vals[:, 0]
    for index in range(1, stream_vals.shape[1]):
        total = total + weights[index] * stream_vals[:, index]
    return total


def remix(stream_vals, mixing, out_scale, delta):
    count = stream_vals.shape[1]
    matrix = jnp.eye(count, dtype=jnp.float32) + mixing
    rows = [
        blend(stream_vals, matrix[:, target]) + out_scale[target] * delta for target in range(count)
    ]
    return jnp.stack(rows, axis=1)


def stream_total(stream_vals):
    total = stream_vals[:, 0]
    for index in range(1, stream_vals.shape[1]):
        total = total + stream_vals[:, index]
    return total


def fold_rows(weight, piece):
    return jnp.dot(piece, weight, preferred_element_type=jnp.float32)


MESH = pl.DeviceIdType.MESH
SLOT_BITS = 6
FILL_BITS = 8


def remote(source, target, send_sem, recv_sem, req):
    return pltpu.make_async_remote_copy(
        src_ref=source,
        dst_ref=target,
        send_sem=send_sem,
        recv_sem=recv_sem,
        device_id={"req": req},
        device_id_type=MESH,
    )


def weigh(tops, totals):
    top = functools.reduce(jnp.maximum, tops)
    factors = [jnp.exp(value - top) for value in tops]
    total = functools.reduce(lambda a, b: a + b, [f * t for f, t in zip(factors, totals)])
    return top, total, factors


def cache_kernel(
    side,
    table,
    last,
    q_ref,
    k_hbm,
    v_hbm,
    num_ref,
    top_ref,
    den_ref,
    q_all,
    k_buf,
    v_buf,
    scores,
    seg_acc,
    seg_top,
    seg_den,
    parts,
    stats,
    relay,
    merged,
    single,
    relay_s,
    merged_s,
    single_s,
    outgoing_s,
    factors,
    small,
    small_s,
    hop,
    hop_s,
    gather_send,
    gather_recv,
    spread_send,
    spread_recv,
    load_sem,
    far_send,
    far_recv,
    near_send,
    near_recv,
    join_send,
    join_recv,
    stat_send,
    stat_recv,
    last_send,
    last_recv,
    last_stat_send,
    last_stat_recv,
):
    block = q_ref.shape[0] // 2
    rows = q_ref.shape[1]
    slots = k_buf.shape[0]
    half_rows = rows // 2
    me = lax.axis_index("req")
    place = (me // side, lax.rem(me, side))
    turn = 1 - 2 * lax.rem(lax.axis_index("head"), 2)

    def shifted(axis, delta):
        moved = lax.rem(place[axis] + side + delta, side)
        return moved * side + place[1] if axis == 0 else place[0] * side + moved

    def at(axis, delta):
        return lax.rem(place[axis] + side + delta, side)

    first = (0, 1)
    second = (1, 0)

    def spot(half, p2, p1):
        return pl.ds(((half * side + p2) * side + p1) * block, block)

    loads = [
        pltpu.make_async_copy(k_hbm, k_buf, load_sem.at[0]),
        pltpu.make_async_copy(v_hbm, v_buf, load_sem.at[1]),
    ]
    for load in loads:
        load.start()
    barrier = pltpu.get_barrier_semaphore()
    for axis in (0, 1):
        for delta in (1, -1):
            pl.semaphore_signal(
                barrier, inc=1, device_id={"req": shifted(axis, delta)}, device_id_type=MESH
            )
    pl.semaphore_wait(barrier, 4)

    sends = []

    def go(copy):
        copy.start()
        sends.append(copy)
        return copy

    def pass_block(half, axis, delta, p2, p1, send, recv, own=False):
        view = q_all.at[spot(half, p2, p1)]
        source = q_ref.at[pl.ds(half * block, block)] if own else view
        return go(remote(source, view, send, recv, shifted(axis, delta)))

    lines = {}
    crosses = {}

    def line(half, index, delta, p1, own=False):
        lines[half, index] = pass_block(
            half, first[half], delta, at(second[half], 0), p1,
            gather_send.at[half, index], gather_recv.at[half, index], own,
        )

    def cross(half, piece, index, delta, p2, p1, own=False):
        crosses[half, piece, index] = pass_block(
            half, second[half], delta, p2, p1,
            spread_send.at[half, piece, index], spread_recv.at[half, piece, index], own,
        )

    halves = (0, 1)
    for half in halves:
        line(half, 0, turn, at(first[half], 0), True)
        line(half, 1, -turn, at(first[half], 0), True)
    for half in halves:
        cross(half, 0, 0, turn, at(second[half], 0), at(first[half], 0), True)
        cross(half, 0, 1, -turn, at(second[half], 0), at(first[half], 0), True)
    for half in halves:
        q_all[spot(half, at(second[half], 0), at(first[half], 0))] = q_ref[
            half * block : (half + 1) * block
        ]
    seg_top[...] = jnp.full(seg_top.shape, NEG_FILL, jnp.float32)
    seg_den[...] = jnp.zeros(seg_den.shape, jnp.float32)
    seg_acc[slots] = jnp.zeros(seg_acc.shape[1:], seg_acc.dtype)
    for half in halves:
        lines[half, 0].wait_recv()
        line(half, 2, turn, at(first[half], -turn))
        cross(half, 1, 0, turn, at(second[half], 0), at(first[half], -turn))
        cross(half, 1, 1, -turn, at(second[half], 0), at(first[half], -turn))
    for half in halves:
        lines[half, 1].wait_recv()
        cross(half, 2, 0, turn, at(second[half], 0), at(first[half], turn))
        cross(half, 2, 1, -turn, at(second[half], 0), at(first[half], turn))
    for half in halves:
        crosses[half, 0, 0].wait_recv()
        cross(half, 0, 2, turn, at(second[half], -turn), at(first[half], 0))
    for half in halves:
        lines[half, 2].wait_recv()
        cross(half, 3, 0, turn, at(second[half], 0), at(first[half], 2))
        cross(half, 3, 1, -turn, at(second[half], 0), at(first[half], 2))
    for piece, delta in ((1, -turn), (2, turn), (3, 2)):
        for half in halves:
            crosses[half, piece, 0].wait_recv()
            cross(half, piece, 2, turn, at(second[half], -turn), at(first[half], delta))
    for piece in range(4):
        for half in halves:
            crosses[half, piece, 1].wait_recv()
            crosses[half, piece, 2].wait_recv()
    for load in loads:
        load.wait()

    slot_mask = (1 << SLOT_BITS) - 1
    fill_mask = (1 << FILL_BITS) - 1
    requests = 2 * block * side * side

    def owner_at(index):
        return table[index] >> (SLOT_BITS + FILL_BITS)

    def starts_new(index):
        before = owner_at(jnp.maximum(index - 1, 0))
        return jnp.logical_or(index == 0, before != owner_at(index))

    shape = (k_buf.shape[1], rows)
    row_ids = lax.broadcasted_iota(jnp.int32, shape, 0)
    col_head = (lax.broadcasted_iota(jnp.int32, shape, 1) >= half_rows).astype(jnp.int32)
    matched = (row_ids & 1) == col_head
    key_ids = row_ids >> 1
    unroll = 4

    def score_step(group, carry):
        for offset in range(unroll):
            index = group * unroll + offset
            entry = table[index]
            fill = (entry >> SLOT_BITS) & fill_mask
            owner = jnp.minimum(entry >> (SLOT_BITS + FILL_BITS), requests - 1)
            home = owner // (2 * block)
            within = lax.rem(owner, 2 * block)
            half = within // block
            hx = home // side
            hy = lax.rem(home, side)
            outer = jnp.where(half == 0, hy, hx)
            inner = jnp.where(half == 0, hx, hy)
            row = ((half * side + outer) * side + inner) * block + lax.rem(within, block)
            found = lax.dot_general(
                k_buf[entry & slot_mask],
                q_all[row],
                (((1,), (1,)), ((), ())),
                preferred_element_type=jnp.float32,
            )
            found = jnp.where(jnp.logical_and(matched, key_ids < fill), found, NEG_FILL)
            scores[index] = found
            seg_top[index, :, 0:rows] = jnp.max(found, axis=0, keepdims=True)
        return carry

    lax.fori_loop(0, slots // unroll, score_step, 0)

    def forward(index, run):
        here = seg_top[index]
        run = jnp.where(starts_new(index), here, jnp.maximum(run, here))
        seg_top[index] = run
        return run

    lax.fori_loop(0, slots, forward, jnp.full(seg_top.shape[1:], NEG_FILL, jnp.float32))

    def backward(step, run):
        index = slots - 1 - step
        follow = jnp.minimum(index + 1, slots - 1)
        ends = jnp.logical_or(step == 0, owner_at(follow) != owner_at(index))
        run = jnp.where(ends, seg_top[index], run)
        seg_top[index] = run
        return run

    lax.fori_loop(0, slots, backward, jnp.full(seg_top.shape[1:], NEG_FILL, jnp.float32))

    def value_step(group, carry):
        acc_run, den_run = carry
        for offset in range(unroll):
            index = group * unroll + offset
            fresh = starts_new(index)
            top = seg_top[index][:, 0:rows]
            top = jnp.where(top < 0.5 * NEG_FILL, 0.0, top)
            weight = jnp.exp(scores[index] - top)
            den = jnp.sum(weight, axis=0, keepdims=True)
            acc = lax.dot_general(
                weight.astype(jnp.bfloat16),
                v_buf[table[index] & slot_mask],
                (((0,), (0,)), ((), ())),
                preferred_element_type=jnp.float32,
            )
            acc_run = acc + jnp.where(fresh, 0.0, acc_run)
            den_run = den + jnp.where(fresh, 0.0, den_run)
            seg_acc[index] = acc_run.astype(seg_acc.dtype)
            seg_den[index, :, 0:rows] = den_run
        return acc_run, den_run

    lax.fori_loop(
        0,
        slots // unroll,
        value_step,
        (jnp.zeros(seg_acc.shape[1:], jnp.float32), jnp.zeros((1, rows), jnp.float32)),
    )

    def place_step(group, carry):
        for piece in range(side):
            tops, dens = [], []
            for offset in range(block):
                spot_index = (group * side + piece) * block + offset
                found = last[spot_index]
                parts[spot_index] = seg_acc[found]
                tops.append(seg_top[found])
                dens.append(seg_den[found])
            stats[group, 0, piece * block : (piece + 1) * block] = jnp.concatenate(tops, axis=0)
            stats[group, 1, piece * block : (piece + 1) * block] = jnp.concatenate(dens, axis=0)
        return carry

    lax.fori_loop(0, 2 * side, place_step, 0)

    def part(half, p2, p1):
        return parts.at[spot(half, p2, p1)]

    def stat(half, p2):
        return stats.at[half * side + p2]

    def combine(put, terms, weights):
        columns = [jnp.transpose(weight) for weight in weights]
        for item in range(block):
            total = None
            for term, column in zip(terms, columns):
                value = term[item].astype(jnp.float32) * column[0:rows, item : item + 1]
                total = value if total is None else total + value
            put(item, total)

    stat_copies = {}
    far, near = {}, {}
    for half in halves:
        up, down = shifted(second[half], turn), shifted(second[half], -turn)
        stat_copies[half, 0] = go(
            remote(stat(half, at(second[half], 2)), relay_s.at[half],
                   stat_send.at[half, 0], stat_recv.at[half, 0], up))
        stat_copies[half, 1] = go(
            remote(stat(half, at(second[half], -turn)), single_s.at[half],
                   stat_send.at[half, 1], stat_recv.at[half, 1], down))
    for order in range(4):
        for half in halves:
            up, down = shifted(second[half], turn), shifted(second[half], -turn)
            p1 = at(first[half], 2 - turn * order)
            far[half, order] = go(
                remote(part(half, at(second[half], 2), p1), relay.at[half, p1],
                       far_send.at[half, order], far_recv.at[half, order], up))
            near[half, order] = go(
                remote(part(half, at(second[half], -turn), p1), single.at[half, p1],
                       near_send.at[half, order], near_recv.at[half, order], down))

    for half in halves:
        stat_copies[half, 0].wait_recv()
        mine = stat(half, at(second[half], turn))
        top, den, weights = weigh([mine[0], relay_s[half, 0]], [mine[1], relay_s[half, 1]])
        outgoing_s[half, 0] = top
        outgoing_s[half, 1] = den
        factors[half, 0] = weights[0]
        factors[half, 1] = weights[1]
        stat_copies[half, 2] = go(
            remote(outgoing_s.at[half], merged_s.at[half],
                   stat_send.at[half, 2], stat_recv.at[half, 2], shifted(second[half], turn)))

    def join_copy(half, order):
        p1 = at(first[half], 2 - turn * order)
        return remote(relay.at[half, p1], merged.at[half, p1],
                      join_send.at[half, order], join_recv.at[half, order],
                      shifted(second[half], turn))

    def far_copy(half, order):
        p1 = at(first[half], 2 - turn * order)
        return remote(part(half, at(second[half], 2), p1), relay.at[half, p1],
                      far_send.at[half, order], far_recv.at[half, order],
                      shifted(second[half], turn))

    def near_copy(half, order):
        p1 = at(first[half], 2 - turn * order)
        return remote(part(half, at(second[half], -turn), p1), single.at[half, p1],
                      near_send.at[half, order], near_recv.at[half, order],
                      shifted(second[half], -turn))

    def relay_step(order, carry):
        for half in halves:
            p1 = at(first[half], 2 + side - turn * order)
            far_copy(half, order).wait_recv()
            lanes = pl.ds(p1 * block, block)
            target = relay.at[half, p1]

            def put(item, value):
                target[item] = value.astype(target.dtype)

            combine(
                put,
                [part(half, at(second[half], turn), p1), target],
                [factors[half, 0, lanes], factors[half, 1, lanes]],
            )
            join_copy(half, order).start()
        return carry

    lax.fori_loop(0, 4, relay_step, 0)

    for half in halves:
        stat_copies[half, 1].wait_recv()
        stat_copies[half, 2].wait_recv()
        mine = stat(half, at(second[half], 0))
        top, den, weights = weigh(
            [mine[0], merged_s[half, 0], single_s[half, 0]],
            [mine[1], merged_s[half, 1], single_s[half, 1]],
        )
        for index in range(3):
            factors[half, index] = weights[index]
        for p1 in range(side):
            small_s[half, p1, 0] = top[p1 * block : (p1 + 1) * block]
            small_s[half, p1, 1] = den[p1 * block : (p1 + 1) * block]

    def gather_piece(half, order):
        p1 = at(first[half], 2 + side - turn * order)
        near_copy(half, order).wait_recv()
        join_copy(half, order).wait_recv()
        lanes = pl.ds(p1 * block, block)
        target = small.at[half, p1]

        def put(item, value):
            target[item] = value.astype(target.dtype)

        combine(
            put,
            [part(half, at(second[half], 0), p1), merged.at[half, p1], single.at[half, p1]],
            [factors[half, index, lanes] for index in range(3)],
        )

    def piece_step(order, carry):
        for half in halves:
            gather_piece(half, order)
        return carry

    tails = {}

    def tail(half, index, source, source_s, delta):
        peer = shifted(first[half], delta)
        tails[half, index] = (
            go(remote(source_s, hop_s.at[half, index],
                      last_stat_send.at[half, index], last_stat_recv.at[half, index], peer)),
            go(remote(source, hop.at[half, index],
                      last_send.at[half, index], last_recv.at[half, index], peer)),
        )

    lax.fori_loop(0, 1, piece_step, 0)
    for half in halves:
        p1 = at(first[half], 2)
        tail(half, 0, small.at[half, p1], small_s.at[half, p1], turn)
    lax.fori_loop(1, 2, piece_step, 0)
    for half in halves:
        p1 = at(first[half], -turn + 2 + 2)
    lax.fori_loop(2, 4, piece_step, 0)
    for half in halves:
        p1 = at(first[half], -turn)
        tail(half, 1, small.at[half, p1], small_s.at[half, p1], -turn)
    for half in halves:
        p1 = at(first[half], turn)
        for copy in tails[half, 0]:
            copy.wait_recv()
        target = small.at[half, p1]
        top, den, weights = weigh(
            [small_s[half, p1, 0], hop_s[half, 0, 0]], [small_s[half, p1, 1], hop_s[half, 0, 1]]
        )
        small_s[half, p1, 0] = top
        small_s[half, p1, 1] = den

        def put(item, value, target=target):
            target[item] = value.astype(target.dtype)

        combine(put, [target, hop.at[half, 0]], weights)
        tail(half, 2, target, small_s.at[half, p1], turn)
    for half in halves:
        p1 = at(first[half], 0)
        for index in (1, 2):
            for copy in tails[half, index]:
                copy.wait_recv()
        top, den, weights = weigh(
            [small_s[half, p1, 0], hop_s[half, 1, 0], hop_s[half, 2, 0]],
            [small_s[half, p1, 1], hop_s[half, 1, 1], hop_s[half, 2, 1]],
        )
        top_ref[half * block : (half + 1) * block] = top
        den_ref[half * block : (half + 1) * block] = den

        def put(item, value, half=half):
            num_ref[half * block + item] = value

        combine(put, [small.at[half, p1], hop.at[half, 1], hop.at[half, 2]], weights)
    for copy in sends:
        copy.wait_send()
    for half in halves:
        for order in range(4):
            join_copy(half, order).wait_send()


def cache_attention(queries, k_pages, v_pages, page_owner, page_fill):
    req_local, rows, head_dim = queries.shape
    slots, keys = k_pages.shape[0], k_pages.shape[1] * k_pages.shape[2]
    devices = lax.axis_size("req")
    side = math.isqrt(devices)
    block = req_local // 2
    requests = req_local * devices
    owner_key = jnp.where(page_owner < 0, requests, page_owner)
    packed = (
        (owner_key << (SLOT_BITS + FILL_BITS))
        | (jnp.where(page_owner < 0, 0, page_fill) << SLOT_BITS)
        | jnp.arange(slots, dtype=jnp.int32)
    )
    rank = jnp.sum((packed[None, :] < packed[:, None]).astype(jnp.int32), axis=1)
    places = jnp.arange(slots, dtype=jnp.int32)
    table = jnp.sum(jnp.where(rank[None, :] == places[:, None], packed[None, :], 0), axis=1)
    spots = jnp.arange(requests, dtype=jnp.int32)
    half = spots // (requests // 2)
    outer = (spots // (block * side)) % side
    inner = (spots // block) % side
    home = jnp.where(half == 0, inner * side + outer, outer * side + inner)
    request = home * req_local + half * block + spots % block
    below = jnp.sum((owner_key[None, :] <= request[:, None]).astype(jnp.int32), axis=1)
    exact = jnp.sum((owner_key[None, :] == request[:, None]).astype(jnp.int32), axis=1)
    last = jnp.where(exact > 0, below - 1, slots)
    bf16, f32 = jnp.bfloat16, jnp.float32
    unit = (2, side, block, rows, head_dim)
    dma = pltpu.SemaphoreType.DMA
    scratch = [
        pltpu.VMEM((requests, rows, head_dim), bf16),
        pltpu.VMEM((slots, keys, head_dim), bf16),
        pltpu.VMEM((slots, keys, head_dim), bf16),
        pltpu.VMEM((slots, keys, rows), f32),
        pltpu.VMEM((slots + 1, rows, head_dim), bf16),
        pltpu.VMEM((slots + 1, 1, 128), f32),
        pltpu.VMEM((slots + 1, 1, 128), f32),
        pltpu.VMEM((requests, rows, head_dim), bf16),
        pltpu.VMEM((2 * side, 2, side * block, 128), f32),
        pltpu.VMEM(unit, bf16),
        pltpu.VMEM(unit, bf16),
        pltpu.VMEM(unit, bf16),
        pltpu.VMEM((2, 2, side * block, 128), f32),
        pltpu.VMEM((2, 2, side * block, 128), f32),
        pltpu.VMEM((2, 2, side * block, 128), f32),
        pltpu.VMEM((2, 2, side * block, 128), f32),
        pltpu.VMEM((2, 3, side * block, 128), f32),
        pltpu.VMEM(unit, bf16),
        pltpu.VMEM((2, side, 2, block, 128), f32),
        pltpu.VMEM((2, 3, block, rows, head_dim), bf16),
        pltpu.VMEM((2, 3, 2, block, 128), f32),
        dma((2, 3)), dma((2, 3)),
        dma((2, 4, 3)), dma((2, 4, 3)),
        dma((2,)),
        dma((2, 4)), dma((2, 4)),
        dma((2, 4)), dma((2, 4)),
        dma((2, 4)), dma((2, 4)),
        dma((2, 3)), dma((2, 3)),
        dma((2, 3)), dma((2, 3)),
        dma((2, 3)), dma((2, 3)),
    ]
    vmem = pl.BlockSpec(memory_space=pltpu.VMEM)
    smem = pl.BlockSpec(memory_space=pltpu.SMEM)
    anywhere = pl.BlockSpec(memory_space=pl.ANY)
    return pl.pallas_call(
        functools.partial(cache_kernel, side),
        out_shape=(
            jax.ShapeDtypeStruct((req_local, rows, head_dim), f32),
            jax.ShapeDtypeStruct((req_local, 128), f32),
            jax.ShapeDtypeStruct((req_local, 128), f32),
        ),
        in_specs=[smem, smem, vmem, anywhere, anywhere],
        out_specs=(vmem, vmem, vmem),
        scratch_shapes=scratch,
        compiler_params=pltpu.CompilerParams(
            collective_id=0, has_side_effects=True, vmem_limit_bytes=56 << 20
        ),
    )(
        table,
        last,
        queries,
        k_pages.reshape(slots, keys, head_dim),
        v_pages.reshape(slots, keys, head_dim),
    )


def transpose_sum(values):
    half = values.shape[1] // 2
    return jnp.sum(jnp.transpose(values[:, 0:half] + values[:, half:]), axis=0, keepdims=True)


def layer_kernel(
    chips,
    chunks,
    hc_in,
    hc_mix,
    hc_out,
    accepted,
    attended,
    streams,
    out_hbm,
    gate_hbm,
    down_hbm,
    fresh_ref,
    final_ref,
    out_buf,
    gate_buf,
    down_buf,
    first_buf,
    mixed_buf,
    total_buf,
    share,
    twin,
    relay,
    joined,
    single,
    stat_all,
    columns,
    normed,
    gathered,
    hidden,
    load_sem,
    own_sem,
    twin_send,
    twin_recv,
    ring_send,
    ring_recv,
    stat_send,
    stat_recv,
    copy_send,
    copy_recv,
    pass_send,
    pass_recv,
):
    tokens, feature = attended.shape
    size = tokens // chunks
    group = 2 * chips
    width = group * feature
    count = streams.shape[0]
    inner = hidden.shape[1]
    strips = inner // feature
    me = lax.axis_index("head")
    chip = me // 2
    core = lax.rem(me, 2)
    turn = 1 - 2 * core

    def at(delta):
        return lax.rem(chip + chips + delta, chips)

    def peer(delta):
        return at(delta) * 2 + core

    sibling = chip * 2 + 1 - core

    def send_to(source, target, send_sem, recv_sem, head):
        return pltpu.make_async_remote_copy(
            src_ref=source,
            dst_ref=target,
            send_sem=send_sem,
            recv_sem=recv_sem,
            device_id={"head": head},
            device_id_type=MESH,
        )

    loads = []
    for index in range(group):
        loads.append(
            pltpu.make_async_copy(
                out_hbm.at[:, pl.ds(index * feature, feature)], out_buf.at[index], load_sem.at[0, index]
            )
        )
    for index in range(2 * strips):
        kind, strip = index // strips, index % strips
        loads.append(
            pltpu.make_async_copy(
                gate_hbm.at[kind, :, pl.ds(strip * feature, feature)],
                gate_buf.at[index],
                load_sem.at[1, index],
            )
        )
    for index in range(group):
        loads.append(
            pltpu.make_async_copy(
                down_hbm.at[:, pl.ds(index * feature, feature)], down_buf.at[index], load_sem.at[2, index]
            )
        )
    for load in loads:
        load.start()
    barrier = pltpu.get_barrier_semaphore()
    for step in range(1, group):
        pl.semaphore_signal(
            barrier, inc=1, device_id={"head": lax.rem(me + step, group)}, device_id_type=MESH
        )
    pl.semaphore_wait(barrier, group - 1)

    sends = []

    def go(copy):
        copy.start()
        sends.append(copy)
        return copy

    offsets = (2, 1, 3, 0)
    waits = {}

    def chunk_rows(t):
        return pl.ds(t * size, size)

    def lanes(head):
        return pl.ds(pl.multiple_of(head * feature, feature), feature)

    def scatter(which, t, product):
        for k, offset in enumerate(offsets):
            target = at(offset)
            piece = share.at[which, t, 1 - core, target]
            piece[...] = product(target * 2 + 1 - core).astype(piece.dtype)
            waits["twin", which, t, k] = go(
                send_to(piece, twin.at[which, t, target], twin_send.at[which, t, k],
                        twin_recv.at[which, t, k], sibling))
        for offset in offsets:
            target = at(offset)
            piece = share.at[which, t, core, target]
            piece[...] = product(target * 2 + core).astype(piece.dtype)

    def widen(ref):
        return ref[...].astype(jnp.float32)

    def chip_sum(which, t):
        def fold(k):
            waits["twin", which, t, k].wait_recv()
            target = at(offsets[k])
            piece = share.at[which, t, core, target]
            piece[...] = (widen(piece) + widen(twin.at[which, t, target])).astype(piece.dtype)

        fold(0)
        waits["far", which, t] = go(
            send_to(share.at[which, t, core, at(2)], relay.at[which, t],
                    ring_send.at[which, t, 0], ring_recv.at[which, t, 0], peer(turn)))
        fold(1)
        fold(2)
        waits["near", which, t] = go(
            send_to(share.at[which, t, core, at(-turn)], single.at[which, t],
                    ring_send.at[which, t, 1], ring_recv.at[which, t, 1], peer(-turn)))
        fold(3)

    def chip_relay(which, t):
        waits["far", which, t].wait_recv()
        piece = relay.at[which, t]
        piece[...] = (widen(piece) + widen(share.at[which, t, core, at(turn)])).astype(piece.dtype)
        waits["join", which, t] = go(
            send_to(piece, joined.at[which, t],
                    ring_send.at[which, t, 2], ring_recv.at[which, t, 2], peer(turn)))

    def finish(which, t):
        waits["near", which, t].wait_recv()
        waits["join", which, t].wait_recv()

    block = 32

    def delta_of(which, t, rows):
        return (
            share[which, t, core, at(0), rows].astype(jnp.float32)
            + joined[which, t, rows].astype(jnp.float32)
            + single[which, t, rows].astype(jnp.float32)
        )

    def remixed(layer, values, delta):
        result = []
        for target in range(count):
            total = hc_out[layer * count + target] * delta
            for source in range(count):
                weight = hc_mix[(layer * count + source) * count + target]
                if source == target:
                    weight = weight + 1.0
                total = total + weight * values[source]
            result.append(total)
        return result

    def project(t):
        if t == 0:
            for load in loads[:group]:
                load.wait()
        values = attended[t * size : (t + 1) * size]
        scatter(0, t, lambda head: jnp.dot(
            values, out_buf[head], preferred_element_type=jnp.float32))

    def middle(t):
        finish(0, t)

        def step(index, carry):
            inside = pl.ds(index * block, block)
            rows = pl.ds(t * size + index * block, block)
            values = [streams[s, rows].astype(jnp.float32) for s in range(count)]
            result = remixed(0, values, delta_of(0, t, inside))
            mixed = None
            for s in range(count):
                first_buf[s, rows] = result[s]
                term = hc_in[count + s] * result[s]
                mixed = term if mixed is None else mixed + term
            mixed_buf[rows] = mixed
            return carry

        lax.fori_loop(0, size // block, step, 0)
        mixed = mixed_buf[t * size : (t + 1) * size]
        stat_all[t, me, 0:1] = transpose_sum(mixed)
        stat_all[t, me, 1:2] = transpose_sum(mixed * mixed)
        stat_all[t, me, 2:8] = jnp.zeros((6, size), jnp.float32)
        for step in range(1, group):
            waits["stat", t, step] = go(
                send_to(stat_all.at[t, me], stat_all.at[t, me], stat_send.at[t, step],
                        stat_recv.at[t, step], lax.rem(me + step, group)))

    def normalized(t):
        for step in range(1, group):
            waits["stat", t, step].wait_recv()
        total = stat_all[t, 0]
        for index in range(1, group):
            total = total + stat_all[t, index]
        center = total[0:1] / width
        scale = lax.rsqrt(total[1:2] / width - center * center + 1e-05)
        row = lax.broadcasted_iota(jnp.int32, total.shape, 0)
        packed = jnp.where(row == 0, center, jnp.where(row == 1, scale, 0.0))
        columns[t] = jnp.transpose(packed)

        def step(index, carry):
            inside = pl.ds(index * block, block)
            rows = pl.ds(t * size + index * block, block)
            column = columns[t, inside]
            value = (mixed_buf[rows] - column[:, 0:1]) * column[:, 1:2]
            normed[rows] = value.astype(normed.dtype)
            return carry

        lax.fori_loop(0, size // block, step, 0)
        mine = normed.at[chunk_rows(t)]
        view = gathered.at[chunk_rows(t), lanes(me)]
        waits["fwd", t] = go(send_to(mine, view, pass_send.at[t, 0], pass_recv.at[t, 0], peer(turn)))
        waits["bwd", t] = go(send_to(mine, view, pass_send.at[t, 1], pass_recv.at[t, 1], peer(-turn)))
        waits["own", t] = go(send_to(mine, view, copy_send.at[t, 0], copy_recv.at[t, 0], sibling))
        local = pltpu.make_async_copy(mine, view, own_sem.at[t])
        local.start()
        waits["local", t] = local

    def hand_over(t, index, delta):
        view = gathered.at[chunk_rows(t), lanes(peer(delta))]
        waits["copy", t, index] = go(
            send_to(view, view, copy_send.at[t, index], copy_recv.at[t, index], sibling))

    def pass_on(t):
        waits["fwd", t].wait_recv()
        view = gathered.at[chunk_rows(t), lanes(peer(-turn))]
        waits["opp", t] = go(send_to(view, view, pass_send.at[t, 2], pass_recv.at[t, 2], peer(turn)))
        hand_over(t, 1, -turn)
        waits["bwd", t].wait_recv()
        hand_over(t, 2, turn)

    def pass_last(t):
        waits["opp", t].wait_recv()
        hand_over(t, 3, 2)

    def feed_forward(t):
        if t == 0:
            for load in loads[group:]:
                load.wait()
        waits["own", t].wait_recv()
        waits["local", t].wait()
        for index in (1, 2, 3):
            waits["copy", t, index].wait_recv()
        values = gathered.at[chunk_rows(t)]
        for strip in range(strips):
            gate = jnp.dot(values[...], gate_buf[strip], preferred_element_type=jnp.float32)
            up = jnp.dot(values[...], gate_buf[strips + strip], preferred_element_type=jnp.float32)
            hidden[:, strip * feature : (strip + 1) * feature] = (
                gate * lax.logistic(gate) * up
            ).astype(hidden.dtype)
        scatter(1, t, lambda head: jnp.dot(
            hidden[...], down_buf[head], preferred_element_type=jnp.float32))

    def last(t):
        finish(1, t)

        def step(index, carry):
            inside = pl.ds(index * block, block)
            rows = pl.ds(t * size + index * block, block)
            values = [first_buf[s, rows] for s in range(count)]
            result = remixed(1, values, delta_of(1, t, inside))
            total = result[0]
            for s in range(count):
                fresh_ref[s, rows] = result[s].astype(fresh_ref.dtype)
                if s > 0:
                    total = total + result[s]
            total_buf[rows] = total
            return carry

        lax.fori_loop(0, size // block, step, 0)

    phases = (
        project,
        lambda t: chip_sum(0, t),
        lambda t: chip_relay(0, t),
        middle,
        normalized,
        pass_on,
        pass_last,
        feed_forward,
        lambda t: chip_sum(1, t),
        lambda t: chip_relay(1, t),
        last,
    )
    for step in range(len(phases) + chunks - 1):
        for t in range(chunks):
            if 0 <= step - t < len(phases):
                phases[step - t](t)
    requests = final_ref.shape[0]
    tree = tokens // requests
    for item in range(requests):
        final_ref[item : item + 1] = total_buf[pl.ds(item * tree + accepted[item], 1)]
    for copy in sends:
        copy.wait_send()


def layer(attended, streams, hc_in, hc_mix, hc_out, out_weight, gate_up, down_weight, accepted):
    tokens, feature = attended.shape
    count = streams.shape[0]
    group = lax.axis_size("head")
    chips = group // 2
    width = out_weight.shape[1]
    inner = down_weight.shape[0]
    strips = inner // feature
    chunks = 3
    size = tokens // chunks
    bf16, f32 = jnp.bfloat16, jnp.float32
    dma = pltpu.SemaphoreType.DMA
    vmem = pl.BlockSpec(memory_space=pltpu.VMEM)
    smem = pl.BlockSpec(memory_space=pltpu.SMEM)
    anywhere = pl.BlockSpec(memory_space=pl.ANY)
    scratch = [
        pltpu.VMEM((group, feature, feature), bf16),
        pltpu.VMEM((2 * strips, width, feature), bf16),
        pltpu.VMEM((group, inner, feature), bf16),
        pltpu.VMEM((count, tokens, feature), f32),
        pltpu.VMEM((tokens, feature), f32),
        pltpu.VMEM((tokens, feature), f32),
        pltpu.VMEM((2, chunks, 2, chips, size, feature), bf16),
        pltpu.VMEM((2, chunks, chips, size, feature), bf16),
        pltpu.VMEM((2, chunks, size, feature), bf16),
        pltpu.VMEM((2, chunks, size, feature), bf16),
        pltpu.VMEM((2, chunks, size, feature), bf16),
        pltpu.VMEM((chunks, group, 8, size), f32),
        pltpu.VMEM((chunks, size, 8), f32),
        pltpu.VMEM((tokens, feature), bf16),
        pltpu.VMEM((tokens, width), bf16),
        pltpu.VMEM((size, inner), bf16),
        dma((3, max(group, 2 * strips))),
        dma((chunks,)),
        dma((2, chunks, 4)), dma((2, chunks, 4)),
        dma((2, chunks, 3)), dma((2, chunks, 3)),
        dma((chunks, group)), dma((chunks, group)),
        dma((chunks, 4)), dma((chunks, 4)),
        dma((chunks, 3)), dma((chunks, 3)),
    ]
    return pl.pallas_call(
        functools.partial(layer_kernel, chips, chunks),
        out_shape=(
            jax.ShapeDtypeStruct((count, tokens, feature), bf16),
            jax.ShapeDtypeStruct((accepted.shape[0], feature), f32),
        ),
        in_specs=[smem] * 4 + [vmem, vmem, anywhere, anywhere, anywhere],
        out_specs=(vmem, vmem),
        scratch_shapes=scratch,
        compiler_params=pltpu.CompilerParams(
            collective_id=1, has_side_effects=True, vmem_limit_bytes=60 << 20
        ),
    )(
        hc_in.reshape(-1),
        hc_mix.reshape(-1),
        hc_out.reshape(-1),
        accepted,
        attended,
        streams,
        out_weight,
        gate_up,
        down_weight,
    )


def on_device(
    streams,
    hc_in,
    hc_mix,
    hc_out,
    qkv_weight,
    out_weight,
    up_gate,
    down_weight,
    draft_weight,
    lm_head,
    k_pages,
    v_pages,
    page_owner,
    page_fill,
    cache_len,
    tree_parent,
    accepted_index,
):
    tokens_local = streams.shape[0]
    feature_local = streams.shape[2]
    width = qkv_weight.shape[0]
    req_local = cache_len.shape[0]
    tree_size = tree_parent.shape[1]
    slot_count = k_pages.shape[0]
    page_size = k_pages.shape[1]
    heads_local = k_pages.shape[2]
    head_dim = k_pages.shape[3]
    draft_count = draft_weight.shape[0]
    all_requests = req_local * lax.axis_size("req")
    reach = ancestors(tree_parent)
    depth = (jnp.sum(reach, axis=2) - 1.0).astype(jnp.int32)
    positions = (cache_len[:, None] + depth).reshape(tokens_local)
    stream_vals = streams.astype(jnp.float32)
    mixed_in = blend(stream_vals, hc_in[0])
    stat_sum, stat_square = lax.psum(
        (jnp.sum(mixed_in, axis=1), jnp.sum(mixed_in * mixed_in, axis=1)), "head"
    )
    normed = normalize(mixed_in, stat_sum[:, None], stat_square[:, None], width).astype(
        jnp.bfloat16
    )
    qkv_flat = qkv_weight.reshape(width, -1)
    normed_full = lax.all_gather(normed, "head", axis=1, tiled=True)
    gate_up = jnp.transpose(up_gate, (1, 0, 2))
    normed_full, gate_up = lax.optimization_barrier((normed_full, gate_up))
    projected = fold_rows(qkv_flat, normed_full)
    projected = projected.reshape(tokens_local, 3, heads_local, head_dim)
    queries = (rotate(projected[:, 0], positions) * head_dim ** (-0.5)).astype(jnp.bfloat16)
    keys_new = rotate(projected[:, 1], positions).astype(jnp.bfloat16)
    values_new = projected[:, 2].astype(jnp.bfloat16)
    query_rows = (
        queries.reshape(req_local, tree_size, heads_local, head_dim)
        .transpose(0, 2, 1, 3)
        .reshape(req_local, heads_local * tree_size, head_dim)
    )
    own_sum, own_top, own_den = cache_attention(
        query_rows, k_pages, v_pages, page_owner, page_fill
    )
    own_sum = own_sum.reshape(req_local, heads_local, tree_size, head_dim).transpose(0, 2, 1, 3)
    used = heads_local * tree_size
    own_top = own_top[:, :used].reshape(req_local, heads_local, tree_size).transpose(0, 2, 1)
    own_den = own_den[:, :used].reshape(req_local, heads_local, tree_size).transpose(0, 2, 1)
    query_own = queries.reshape(req_local, tree_size, heads_local, head_dim)
    keys_own = keys_new.reshape(req_local, tree_size, heads_local, head_dim)
    values_own = values_new.reshape(req_local, tree_size, heads_local, head_dim)
    tree_scores = jnp.einsum(
        "jqhd,jkhd->jqhk", query_own, keys_own, preferred_element_type=jnp.float32
    )
    tree_mask = (reach > 0)[:, :, None, :]
    tree_scores = jnp.where(tree_mask, tree_scores, NEG_FILL)
    top = jnp.maximum(own_top, jnp.max(tree_scores, axis=3))
    carried = jnp.exp(own_top - top)
    tree_weights = jnp.where(tree_mask, jnp.exp(tree_scores - top[..., None]), 0.0)
    denominator = own_den * carried + jnp.sum(tree_weights, axis=3)
    numerator = own_sum * carried[..., None] + jnp.einsum(
        "jqhk,jkhd->jqhd",
        tree_weights.astype(jnp.bfloat16),
        values_own,
        preferred_element_type=jnp.float32,
    )
    attended = (
        (numerator / denominator[..., None])
        .astype(jnp.bfloat16)
        .reshape(tokens_local, heads_local * head_dim)
    )
    fresh, final_local = layer(
        attended,
        jnp.transpose(streams, (1, 0, 2)),
        hc_in,
        hc_mix,
        hc_out,
        out_weight,
        gate_up,
        down_weight,
        accepted_index,
    )
    new_streams = jnp.transpose(fresh, (1, 0, 2))
    final_full = lax.all_gather(final_local, "head", axis=1, tiled=True)
    final_norm = layer_norm(final_full)
    own_columns = lax.dynamic_slice_in_dim(
        final_norm, lax.axis_index("head") * feature_local, feature_local, 1
    )
    branch = jnp.einsum(
        "jd,kde->jke",
        final_norm.astype(jnp.bfloat16),
        draft_weight,
        preferred_element_type=jnp.float32,
    )
    drafted = (own_columns[:, None, :] + jax.nn.silu(branch)).astype(jnp.bfloat16)
    draft_full = lax.all_gather(drafted, "head", axis=2, tiled=True)
    draft_all = lax.all_gather(draft_full, "req", axis=0, tiled=True)
    logits_local = jnp.dot(
        draft_all.reshape(-1, width), lm_head, preferred_element_type=jnp.float32
    )
    logits_local = logits_local.reshape(all_requests, draft_count, -1)
    logits = lax.all_to_all(
        logits_local.astype(jnp.bfloat16), ("req", "head"), split_axis=0, concat_axis=2, tiled=True
    ).astype(logits_local.dtype)
    return (new_streams, logits)


def solution(mesh):
    in_specs = (
        P("req", None, "head"),
        P(),
        P(),
        P(),
        P(None, None, "head"),
        P("head", None),
        P(None, None, "head"),
        P("head", None),
        P(None, None, "head"),
        P(None, ("req", "head")),
        P("req", None, "head", None),
        P("req", None, "head", None),
        P("req"),
        P("req"),
        P("req"),
        P("req", None),
        P("req"),
    )
    out_specs = (P("req", None, "head"), P(("req", "head"), None, None))
    return jax.shard_map(
        on_device, mesh=mesh, in_specs=in_specs, out_specs=out_specs, check_vma=False
    )
```

profile of v0, /device:TPU:1, one launch (start us, length us, event | category | flops | bytes accessed | tf_op | source)
XLA Modules:
  0.0 349.6 jit_solution(17807104673093564240)
XLA Ops:
  7.2 1.5 fusion.55
  8.8 2.9 copy_bitcast_fusion.1
  11.7 2.8 fusion.53
  14.7 14.7 %all-reduce = (f32[768]{0:T(1024)S(1)}, f32[768]{0:T(1024)S(1)}) all-reduce(f32[768]{0:T(1024)S(1)} %fusion.17, f32[768]{0:T(1024)S(1)} %get-tuple-element.32), channel_id=1, replica_groups=mesh['req'=16,'head'=8] {'head'}, use_global_device_ids=true, to_apply=%region_7.8 | all-reduce | flops 1536 | bytes 12288 | tf_op jit(solution)/shard_map/psum | solution.py:1062
  29.4 1.0 fusion.16
  31.1 9.3 %copy.94 = bf16[2048,2,1024]{2,0,1:T(8,128)(2,1)} copy(bf16[2048,2,1024]{2,1,0:T(2,128)(2,1)} %param.23) | data formatting | bytes 16777216 | tf_op args[6]
  40.4 5.3 %copy.67 = bf16[2048,3,256]{0,2,1:T(8,128)(2,1)} copy(bf16[2048,3,256]{2,0,1:T(8,128)(2,1)} %param.21) | data formatting | bytes 6291456 | tf_op args[4]
  49.2 0.8 copy.72
  53.7 10.4 %all-gather.3.cloned.1.call-done = bf16[768,2048]{1,0:T(8,128)(2,1)} async-done(((bf16[768,256]{1,0:T(8,128)(2,1)}), bf16[768,2048]{1,0:T(8,128)(2,1)}) %all-gather.3.cloned.1.call-update) | async-done | bytes 3145744 | tf_op jit(solution)/shard_map/all_gather | solution.py:1069
  64.1 5.5 %fusion = f32[768,3,2,128]{0,3,2,1:T(8,128)S(1)} fusion(bf16[3,2,128,2048]{3,2,1,0:T(8,128)(2,1)} %bitcast.115, bf16[768,2048]{1,0:T(8,128)(2,1)} %all-gather.3.cloned.1.call-done), kind=kOutput, calls=%fused_computation.1 | convolution fusion | flops 2415919104 | bytes 8650752 | tf_op jit(solution)/shard_map/dot_general | solution.py:77
  70.5 1.0 subtract_convert_fusion
  71.5 1.5 concatenate.17
  73.1 1.4 copy.70
  75.0 1.3 copy.71
  76.4 1.6 concatenate.20
  78.0 1.2 copy.73
  79.2 1.5 concatenate.21
  80.8 1.2 copy.74
  82.0 2.2 fusion.14
  84.2 87.0 %shard_map.176 = (f32[16,96,128]{2,1,0:T(8,128)}, f32[16,128]{1,0:T(8,128)}, f32[16,128]{1,0:T(8,128)}) custom-call(s32[48]{0:T(128)} %select_reduce_fusion.table, s32[256]{0:T(256)} %compare_select_fusion.6.last, bf16[16,96,128]{2,1,0:T(8,128)(2,1)} %bitcast.112, bf16[48,256,128]{2,1,0:T(8,128)(2,1)} %bitcast.113, bf16[48,256,128]{2,1,0:T(8,128)(2,1)} %bitcast.114), custom_call_target="tpu_custom_call" | custom-call | tf_op jit(solution)/shard_map/pallas_call | solution.py:606
  172.7 0.9 copy.75
  173.7 1.5 fusion.57
  177.3 65.9 %shard_map.177 = (bf16[4,768,256]{2,1,0:T(8,128)(2,1)}, f32[16,256]{1,0:T(8,128)}) custom-call(f32[8]{0:T(128)} %reshape.267.hc_in, f32[32]{0:T(128)} %reshape.268.hc_mix, f32[8]{0:T(128)} %reshape.269.hc_out, s32[16]{0:T(128)} %accepted.1, bf16[768,256]{1,0:T(8,128)(2,1)} %bitcast.119, bf16[4,768,256]{2,1,0:T(8,128)(2,1)} %get-tuple-element.36.streams, ...), custom_call_target="tpu_custom_call" | custom-call | tf_op jit(solution)/shard_map/pallas_call | solution.py:1002
  243.2 14.5 %all_gather.13 = f32[16,2048]{1,0:T(8,128)S(1)} all-gather(f32[16,256]{1,0:T(8,128)} %get-tuple-element.15), channel_id=1, replica_groups=mesh['req'=16,'head'=8] {'head'}, dimensions={1}, use_global_device_ids=true | all-gather | bytes 147456 | tf_op jit(solution)/shard_map/all_gather | solution.py:1124
  258.4 14.2 %all_gather.14 = bf16[16,2,2048]{2,0,1:T(8,128)(2,1)} all-gather(bf16[16,2,256]{2,0,1:T(8,128)(2,1)S(1)} %add_convert_fusion.1), channel_id=1, replica_groups=mesh['req'=16,'head'=8] {'head'}, dimensions={2}, use_global_device_ids=true | all-gather | bytes 147456 | tf_op jit(solution)/shard_map/all_gather | solution.py:1136
  272.6 40.6 %all-gather.5.cloned.1.call-done = bf16[256,2,2048]{2,0,1:T(8,128)(2,1)} async-done(((bf16[16,2,2048]{2,0,1:T(8,128)(2,1)}), bf16[256,2,2048]{2,0,1:T(8,128)(2,1)}) %all-gather.5.cloned.1.call-update) | async-done | bytes 2097168 | tf_op jit(solution)/shard_map/all_gather | solution.py:1137
  313.2 3.1 fusion.7
  316.3 1.2 copy.80
  317.5 8.5 %all-to-all-start = ((bf16[256,2,393]{2,1,0:T(2,128)(2,1)}), bf16[256,2,393]{2,1,0:T(2,128)(2,1)S(1)}, u32[]{:S(2)}, u32[]{:S(2)}) async-start(bf16[256,2,393]{2,1,0:T(2,128)(2,1)} %copy.80), calls=%async_computation | async-start | bytes 1048576 | tf_op jit(solution)/shard_map/all_to_all | solution.py:1142
  326.0 3.8 %copy.82 = bf16[768,4,256]{2,1,0:T(4,128)(2,1)} copy(bf16[768,4,256]{2,0,1:T(8,128)(2,1)} %bitcast.117) | data formatting | bytes 3145728
  329.7 9.9 %all-to-all-done = bf16[256,2,393]{2,1,0:T(2,128)(2,1)S(1)} async-done(((bf16[256,2,393]{2,1,0:T(2,128)(2,1)}), bf16[256,2,393]{2,1,0:T(2,128)(2,1)S(1)}, u32[]{:S(2)}, u32[]{:S(2)}) %all-to-all-start) | async-done | bytes 402464 | tf_op jit(solution)/shard_map/all_to_all | solution.py:1142
  340.4 2.1 reshape.278
  (75 shorter events, 14.5 us)
Async XLA Ops:
  7.2 250.8 %copy-start = (bf16[2,2048,256]{2,1,0:T(8,128)(2,1)S(1)}, bf16[2,2048,256]{2,1,0:T(8,128)(2,1)}, u32[]{:S(2)}) copy-start(bf16[2,2048,256]{2,1,0:T(8,128)(2,1)} %param.25) | copy-start | bytes 6291460
  7.2 56.9 %all-gather.3.cloned.1.call-start = ((), (), s32[]{:S(2)}) async-start(), calls=%async_computation.1 | async-start | bytes 3538944 | tf_op jit(solution)/shard_map/all_gather | solution.py:1069
  11.7 18.8 %copy-start.8 = (f32[2,4]{1,0:T(2,128)S(1)}, f32[2,4]{1,0:T(2,128)}, u32[]{:S(2)}) copy-start(f32[2,4]{1,0:T(2,128)} %param.18) | copy-start | bytes 100
  30.4 282.8 %all-gather.5.cloned.1.call-start = ((), (), s32[]{:S(2)}) async-start(), calls=%async_computation.2 | async-start | bytes 2228224 | tf_op jit(solution)/shard_map/all_gather | solution.py:1137
  40.4 5.3 %copy-start.13 = (s32[16,48]{1,0:T(8,128)S(1)}, s32[16,48]{1,0:T(8,128)}, u32[]{:S(2)}) copy-start(s32[16,48]{1,0:T(8,128)} %param.32) | copy-start | bytes 9220
  46.6 2.3 copy-start.9
  47.2 2.8 copy-start.7
  47.2 3.5 copy-start.14
  47.2 4.1 %copy-start.10 = (s32[48]{0:T(128)S(1)}, s32[48]{0:T(128)}, u32[]{:S(2)}) copy-start(s32[48]{0:T(128)} %param.29) | copy-start | bytes 580
  47.2 4.1 %copy-start.11 = (s32[48]{0:T(128)S(1)}, s32[48]{0:T(128)}, u32[]{:S(2)}) copy-start(s32[48]{0:T(128)} %param.30) | copy-start | bytes 580
  76.4 5.6 %copy-start.2 = (f32[16,48,2,64]{3,1,2,0:T(8,128)S(1)}, f32[16,48,2,64]{3,1,2,0:T(8,128)}, u32[]{:S(2)}) copy-start(f32[16,48,2,64]{3,1,2,0:T(8,128)} %copy.70) | copy-start | bytes 1179652
  84.2 88.5 %copy-start.3 = (bf16[768,1,2,128]{0,3,2,1:T(8,128)(2,1)S(1)}, bf16[768,1,2,128]{0,3,2,1:T(8,128)(2,1)}, u32[]{:S(2)}) copy-start(bf16[768,1,2,128]{0,3,2,1:T(8,128)(2,1)} %slice.116) | copy-start | bytes 1179652
  84.2 89.5 %copy-start.1 = (bf16[16,48,2,128]{3,1,2,0:T(8,128)(2,1)S(1)}, bf16[16,48,2,128]{3,1,2,0:T(8,128)(2,1)}, u32[]{:S(2)}) copy-start(bf16[16,48,2,128]{3,1,2,0:T(8,128)(2,1)} %fusion.14) | copy-start | bytes 1179652
  84.2 89.5 %copy-start.4 = (bf16[16,48,2,64]{3,1,2,0:T(8,128)(2,1)S(1)}, bf16[16,48,2,64]{3,1,2,0:T(8,128)(2,1)}, u32[]{:S(2)}) copy-start(bf16[16,48,2,64]{3,1,2,0:T(8,128)(2,1)} %copy.73) | copy-start | bytes 589828
  84.2 89.5 %copy-start.5 = (pred[16,48,48]{1,2,0:T(8,128)(4,1)S(1)}, pred[16,48,48]{1,2,0:T(8,128)(4,1)}, u32[]{:S(2)}) copy-start(pred[16,48,48]{1,2,0:T(8,128)(4,1)} %copy.72) | copy-start | bytes 110596
  173.6 1.9 copy-start.6
  173.6 1.9 copy-start.12
  317.5 22.2 %all-to-all-start = ((bf16[256,2,393]{2,1,0:T(2,128)(2,1)}), bf16[256,2,393]{2,1,0:T(2,128)(2,1)S(1)}, u32[]{:S(2)}, u32[]{:S(2)}) async-start(bf16[256,2,393]{2,1,0:T(2,128)(2,1)} %copy.80), calls=%async_computation | async-start | bytes 1048576 | tf_op jit(solution)/shard_map/all_to_all | solution.py:1142
Sparse Core Ops, SparseCore 0:
  30.5 33.4 all-gather.2
  272.7 40.4 all-gather.4
where the time goes:
time: 354 us; the launch traced here: 350 us
  Pallas kernels  153 us (43%)
  waiting for transfers between devices  60.9 us (17%)
  blocking collectives  43.4 us (12%)
  local copies, waits for them, and re-layouts  41.4 us (12%)
  between operations  14.7 us (4%)
  matrix products  14.3 us (4%)
  other arithmetic  13.5 us (4%)
  starting transfers between devices  8.59 us (2%)
    pallas_call x1, Pallas kernels, cache_attention(): pl.pallas_call(functools.partial(cache_kernel, side), out_shape=(jax.Shap...  87 us
    pallas_call x1, Pallas kernels, layer(): pl.pallas_call(functools.partial(layer_kernel, chips, chunks), out_shape=...  65.9 us
    all_gather x1, waiting for transfers between devices, on_device(): draft_all = lax.all_gather(draft_full, 'req', axis=0, tiled=True)  40.6 us
    unnamed x34, local copies, waits for them, and re-layouts  19.2 us
    psum x1, blocking collectives, on_device(): lax.psum((jnp.sum(mixed_in, axis=1), jnp.sum(mixed_in * mixed_in, axis=1)...  14.7 us
    all_gather x1, blocking collectives, on_device(): final_full = lax.all_gather(final_local, 'head', axis=1, tiled=True)  14.5 us
    all_gather x1, blocking collectives, on_device(): draft_full = lax.all_gather(drafted, 'head', axis=2, tiled=True)  14.2 us
    concatenate x8, local copies, waits for them, and re-layouts, rotate(): jnp.concatenate([first * cosine - second * sine, second * cosine + first...  10.4 us
  transfers between devices with their start and end apart: 3, of which 3 were waited for; matrix products, arithmetic and copies ran while one was open for 8% of the time, Pallas kernels for 0%

commit v1 on v0

--- a/solution.py
+++ b/solution.py
@@ -951,15 +951,21 @@
         for t in range(chunks):
             if 0 <= step - t < len(phases):
                 phases[step - t](t)
-    requests = final_ref.shape[0]
+    requests = accepted.shape[0]
+    repeats = final_ref.shape[0] // requests
     tree = tokens // requests
     for item in range(requests):
-        final_ref[item : item + 1] = total_buf[pl.ds(item * tree + accepted[item], 1)]
+        row = total_buf[pl.ds(item * tree + accepted[item], 1)]
+        for copy_index in range(repeats):
+            place = item * repeats + copy_index
+            final_ref[place : place + 1] = row
     for copy in sends:
         copy.wait_send()
 
 
-def layer(attended, streams, hc_in, hc_mix, hc_out, out_weight, gate_up, down_weight, accepted):
+def layer(
+    attended, streams, hc_in, hc_mix, hc_out, out_weight, gate_up, down_weight, accepted, repeats
+):
     tokens, feature = attended.shape
     count = streams.shape[0]
     group = lax.axis_size("head")
@@ -1003,7 +1009,7 @@
         functools.partial(layer_kernel, chips, chunks),
         out_shape=(
             jax.ShapeDtypeStruct((count, tokens, feature), bf16),
-            jax.ShapeDtypeStruct((accepted.shape[0], feature), f32),
+            jax.ShapeDtypeStruct((accepted.shape[0] * repeats, feature), f32),
         ),
         in_specs=[smem] * 4 + [vmem, vmem, anywhere, anywhere, anywhere],
         out_specs=(vmem, vmem),
@@ -1022,6 +1028,209 @@
         gate_up,
         down_weight,
     )
+
+
+def draft_kernel(
+    chips,
+    final_ref,
+    weight_hbm,
+    vocab_hbm,
+    logits_ref,
+    final_all,
+    weight_buf,
+    vocab_buf,
+    gathered,
+    total,
+    load_sem,
+    sum_send,
+    sum_recv,
+    draft_send,
+    draft_recv,
+    copy_send,
+    copy_recv,
+    pass_send,
+    pass_recv,
+):
+    rows, feature = final_ref.shape
+    group = 2 * chips
+    width = group * feature
+    devices = gathered.shape[1] // rows
+    me = lax.axis_index("head")
+    home = lax.axis_index("req")
+    chip = me // 2
+    core = lax.rem(me, 2)
+    turn = 1 - 2 * core
+    sibling = chip * 2 + 1 - core
+
+    def peer(delta):
+        return lax.rem(chip + chips + delta, chips) * 2 + core
+
+    def send_to(source, target, send_sem, recv_sem, device):
+        return pltpu.make_async_remote_copy(
+            src_ref=source,
+            dst_ref=target,
+            send_sem=send_sem,
+            recv_sem=recv_sem,
+            device_id=device,
+            device_id_type=MESH,
+        )
+
+    loads = [pltpu.make_async_copy(weight_hbm, weight_buf, load_sem.at[0])]
+    for index in range(group):
+        loads.append(
+            pltpu.make_async_copy(
+                vocab_hbm.at[:, pl.ds(index * feature, feature)],
+                vocab_buf.at[index],
+                load_sem.at[1 + index],
+            )
+        )
+    for load in loads:
+        load.start()
+    barrier = pltpu.get_barrier_semaphore()
+    for step in range(1, group):
+        pl.semaphore_signal(
+            barrier, inc=1, device_id={"head": lax.rem(me + step, group)}, device_id_type=MESH
+        )
+    for step in range(1, devices):
+        pl.semaphore_signal(
+            barrier, inc=1, device_id={"req": lax.rem(home + step, devices)}, device_id_type=MESH
+        )
+    pl.semaphore_wait(barrier, group + devices - 2)
+
+    sends = []
+
+    def go(copy):
+        copy.start()
+        sends.append(copy)
+        return copy
+
+    sums = []
+    for step in range(1, group):
+        sums.append(
+            go(send_to(final_ref, final_all.at[me], sum_send.at[step], sum_recv.at[step],
+                       {"head": lax.rem(me + step, group)}))
+        )
+    final_all[me] = final_ref[...]
+    loads[0].wait()
+    for copy in sums:
+        copy.wait_recv()
+    center = jnp.zeros((rows, 1), jnp.float32)
+    square = jnp.zeros((rows, 1), jnp.float32)
+    for index in range(group):
+        values = final_all[index]
+        center = center + jnp.sum(values, axis=1, keepdims=True)
+        square = square + jnp.sum(values * values, axis=1, keepdims=True)
+    center = center / width
+    scale = lax.rsqrt(square / width - center * center + 1e-05)
+    branches = []
+    for kind in range(2):
+        branch = jnp.zeros((rows, feature), jnp.float32)
+        for index in range(group):
+            values = ((final_all[index] - center) * scale).astype(jnp.bfloat16)
+            branch = branch + jnp.dot(
+                values,
+                weight_buf[kind, index * feature : (index + 1) * feature],
+                preferred_element_type=jnp.float32,
+            )
+        branches.append(branch)
+    odd = (lax.broadcasted_iota(jnp.int32, (rows, feature), 0) & 1) == 1
+    branch = jnp.where(odd, branches[1], branches[0])
+    drafted = (final_ref[...] - center) * scale + branch * lax.logistic(branch)
+    mine = gathered.at[me, pl.ds(pl.multiple_of(home * rows, rows), rows)]
+    mine[...] = drafted.astype(gathered.dtype)
+    drafts = []
+    for step in range(1, devices):
+        drafts.append(
+            go(send_to(mine, mine, draft_send.at[step], draft_recv.at[step],
+                       {"req": lax.rem(home + step, devices)}))
+        )
+    for copy in drafts:
+        copy.wait_recv()
+
+    def shard(head):
+        return gathered.at[head]
+
+    def ring(index, delta, source):
+        return go(send_to(shard(source), shard(source), pass_send.at[index], pass_recv.at[index],
+                          {"head": peer(delta)}))
+
+    def hand_over(index, source):
+        return go(send_to(shard(source), shard(source), copy_send.at[index], copy_recv.at[index],
+                          {"head": sibling}))
+
+    fwd = ring(0, turn, me)
+    bwd = ring(1, -turn, me)
+    hands = [hand_over(0, me)]
+    for load in loads[1:]:
+        load.wait()
+
+    def add(head, first=False):
+        value = lax.dot_general(
+            gathered[head],
+            vocab_buf[head],
+            (((1,), (1,)), ((), ())),
+            preferred_element_type=jnp.float32,
+        )
+        total[...] = value if first else total[...] + value
+
+    add(me, True)
+    fwd.wait_recv()
+    opp = ring(2, turn, peer(-turn))
+    hands.append(hand_over(1, peer(-turn)))
+    bwd.wait_recv()
+    hands.append(hand_over(2, peer(turn)))
+    add(peer(-turn))
+    hands[0].wait_recv()
+    add(sibling)
+    add(peer(turn))
+    opp.wait_recv()
+    hands.append(hand_over(3, peer(2)))
+    hands[1].wait_recv()
+
+    def across(delta):
+        return lax.rem(chip + chips + delta, chips) * 2 + 1 - core
+
+    add(across(turn))
+    hands[2].wait_recv()
+    add(across(-turn))
+    add(peer(2))
+    hands[3].wait_recv()
+    add(across(2))
+    logits_ref[...] = total[...].astype(logits_ref.dtype)
+    for copy in sends:
+        copy.wait_send()
+
+
+def draft_logits(final_rows, draft_weight, lm_head):
+    rows, feature = final_rows.shape
+    group = lax.axis_size("head")
+    devices = lax.axis_size("req")
+    width, vocab = lm_head.shape
+    bf16, f32 = jnp.bfloat16, jnp.float32
+    dma = pltpu.SemaphoreType.DMA
+    vmem = pl.BlockSpec(memory_space=pltpu.VMEM)
+    anywhere = pl.BlockSpec(memory_space=pl.ANY)
+    return pl.pallas_call(
+        functools.partial(draft_kernel, group // 2),
+        out_shape=jax.ShapeDtypeStruct((devices * rows, vocab), bf16),
+        in_specs=[vmem, anywhere, anywhere],
+        out_specs=vmem,
+        scratch_shapes=[
+            pltpu.VMEM((group, rows, feature), f32),
+            pltpu.VMEM(draft_weight.shape, bf16),
+            pltpu.VMEM((group, vocab, feature), bf16),
+            pltpu.VMEM((group, devices * rows, feature), bf16),
+            pltpu.VMEM((devices * rows, vocab), f32),
+            dma((1 + group,)),
+            dma((group,)), dma((group,)),
+            dma((devices,)), dma((devices,)),
+            dma((4,)), dma((4,)),
+            dma((3,)), dma((3,)),
+        ],
+        compiler_params=pltpu.CompilerParams(
+            collective_id=2, has_side_effects=True, vmem_limit_bytes=40 << 20
+        ),
+    )(final_rows, draft_weight, jnp.transpose(lm_head))
 
 
 def on_device(
@@ -1119,29 +1328,14 @@
         gate_up,
         down_weight,
         accepted_index,
+        draft_count,
     )
     new_streams = jnp.transpose(fresh, (1, 0, 2))
-    final_full = lax.all_gather(final_local, "head", axis=1, tiled=True)
-    final_norm = layer_norm(final_full)
-    own_columns = lax.dynamic_slice_in_dim(
-        final_norm, lax.axis_index("head") * feature_local, feature_local, 1
-    )
-    branch = jnp.einsum(
-        "jd,kde->jke",
-        final_norm.astype(jnp.bfloat16),
-        draft_weight,
-        preferred_element_type=jnp.float32,
-    )
-    drafted = (own_columns[:, None, :] + jax.nn.silu(branch)).astype(jnp.bfloat16)
-    draft_full = lax.all_gather(drafted, "head", axis=2, tiled=True)
-    draft_all = lax.all_gather(draft_full, "req", axis=0, tiled=True)
-    logits_local = jnp.dot(
-        draft_all.reshape(-1, width), lm_head, preferred_element_type=jnp.float32
-    )
+    logits_local = draft_logits(final_local, draft_weight, lm_head)
     logits_local = logits_local.reshape(all_requests, draft_count, -1)
     logits = lax.all_to_all(
-        logits_local.astype(jnp.bfloat16), ("req", "head"), split_axis=0, concat_axis=2, tiled=True
-    ).astype(logits_local.dtype)
+        logits_local, ("req", "head"), split_axis=0, concat_axis=2, tiled=True
+    ).astype(jnp.float32)
     return (new_streams, logits)
 
 

time: 354 us -> 302 us (0.85)
  waiting for transfers between devices: 60.9 us -> 18.9 us
  Pallas kernels: 153 us -> 184 us
  blocking collectives: 43.4 us -> 14.7 us
  matrix products: 14.3 us -> 8.78 us
  local copies, waits for them, and re-layouts: 41.4 us -> 37.6 us
    all_gather x1 -> x0, waiting for transfers between devices: 40.6 us -> none  [on_device(): draft_all = lax.all_gather(draft_full, 'req', axis=0, tiled=True)]
    pallas_call x0 -> x1, Pallas kernels: none -> 30.8 us  [draft_logits(): pl.pallas_call(functools.partial(draft_kernel, group // 2), out_shape=jax...]
    all_gather x2 -> x0, blocking collectives: 28.7 us -> none  [the longest x1 14.5 us: on_device(): final_full = lax.all_gather(final_local, 'head', axis=1, tiled=True)]
    concatenate x8, local copies, waits for them, and re-layouts: 10.4 us -> 6.09 us  [rotate(): jnp.concatenate([first * cosine - second * sine, second * cosine + first...]
    unnamed x34 -> x30, local copies, waits for them, and re-layouts: 19.2 us -> 20.7 us
  transfers between devices with their start and end apart: 3 -> 2, of which waited for: 3 -> 2; matrix products, arithmetic and copies ran while one was open for 8% -> 9% of each run, Pallas kernels for 0% -> 0%
where the time goes in v1:
time: 302 us; the launch traced here: 298 us
  Pallas kernels  184 us (61%)
  local copies, waits for them, and re-layouts  37.6 us (12%)
  waiting for transfers between devices  18.9 us (6%)
  blocking collectives  14.7 us (5%)
  between operations  14.6 us (5%)
  other arithmetic  13.6 us (5%)
  matrix products  8.78 us (3%)
  starting transfers between devices  5.9 us (2%)
    pallas_call x1, Pallas kernels, cache_attention(): pl.pallas_call(functools.partial(cache_kernel, side), out_shape=(jax.Shap...  86.9 us
    pallas_call x1, Pallas kernels, layer(): pl.pallas_call(functools.partial(layer_kernel, chips, chunks), out_shape=...  65.9 us
    pallas_call x1, Pallas kernels, draft_logits(): pl.pallas_call(functools.partial(draft_kernel, group // 2), out_shape=jax...  30.8 us
    unnamed x30, local copies, waits for them, and re-layouts  20.7 us
    psum x1, blocking collectives, on_device(): lax.psum((jnp.sum(mixed_in, axis=1), jnp.sum(mixed_in * mixed_in, axis=1)...  14.7 us
    all_to_all x1, waiting for transfers between devices, on_device(): lax.all_to_all(logits_local, ('req', 'head'), split_axis=0, concat_axis=2...  9.91 us
    all_gather x1, waiting for transfers between devices, on_device(): normed_full = lax.all_gather(normed, 'head', axis=1, tiled=True)  8.97 us
    concatenate x8, local copies, waits for them, and re-layouts, rotate(): jnp.concatenate([first * cosine - second * sine, second * cosine + first...  6.09 us
  transfers between devices with their start and end apart: 2, of which 2 were waited for; matrix products, arithmetic and copies ran while one was open for 9% of the time, Pallas kernels for 0%

profile of v1, /device:TPU:1, one launch (start us, length us, event | category | flops | bytes accessed | tf_op | source)
XLA Modules:
  0.0 297.8 jit_solution(2957085613947467955)
XLA Ops:
  7.2 1.4 fusion.44
  8.7 2.9 copy_bitcast_fusion.1
  11.6 2.7 fusion.42
  14.5 14.7 %all-reduce = (f32[768]{0:T(1024)S(1)}, f32[768]{0:T(1024)S(1)}) all-reduce(f32[768]{0:T(1024)S(1)} %fusion.12, f32[768]{0:T(1024)S(1)} %get-tuple-element.28), channel_id=1, replica_groups=mesh['req'=16,'head'=8] {'head'}, use_global_device_ids=true, to_apply=%region_7.8 | all-reduce | flops 1536 | bytes 12288 | tf_op jit(solution)/shard_map/psum | solution.py:1271
  29.2 1.0 fusion.11
  30.9 9.4 %copy.75 = bf16[2048,2,1024]{2,0,1:T(8,128)(2,1)} copy(bf16[2048,2,1024]{2,1,0:T(2,128)(2,1)} %param.23) | data formatting | bytes 16777216 | tf_op args[6]
  40.3 3.6 %copy.48 = bf16[2048,3,256]{0,2,1:T(8,128)(2,1)} copy(bf16[2048,3,256]{2,0,1:T(8,128)(2,1)S(1)} %copy-done.4) | data formatting | bytes 6291456 | tf_op args[4]
  47.3 0.7 broadcast_compare_fusion
  48.0 1.1 copy.53
  49.8 1.3 reshape.249.hc_out
  52.0 0.7 select_reduce_fusion.table
  53.4 1.5 multiply_cosine_fusion
  54.9 9.0 %all-gather.2.cloned.1.call-done = bf16[768,2048]{1,0:T(8,128)(2,1)} async-done(((bf16[768,256]{1,0:T(8,128)(2,1)}), bf16[768,2048]{1,0:T(8,128)(2,1)}) %all-gather.2.cloned.1.call-update) | async-done | bytes 3145744 | tf_op jit(solution)/shard_map/all_gather | solution.py:1278
  63.9 4.5 %fusion = f32[768,3,2,128]{0,3,2,1:T(8,128)S(1)} fusion(bf16[3,2,128,2048]{3,2,1,0:T(8,128)(2,1)S(1)} %bitcast.107, bf16[768,2048]{1,0:T(8,128)(2,1)} %all-gather.2.cloned.1.call-done), kind=kOutput, calls=%fused_computation.1 | convolution fusion | flops 2415919104 | bytes 8650752 | tf_op jit(solution)/shard_map/dot_general | solution.py:77
  68.6 0.7 copy-done.6
  69.4 0.9 subtract_convert_fusion
  72.4 1.6 concatenate.20
  74.4 1.6 concatenate.21
  76.5 1.0 fusion.9
  77.5 86.9 %shard_map.176 = (f32[16,96,128]{2,1,0:T(8,128)}, f32[16,128]{1,0:T(8,128)}, f32[16,128]{1,0:T(8,128)}) custom-call(s32[48]{0:T(128)} %select_reduce_fusion.table, s32[256]{0:T(256)} %compare_select_fusion.6.last, bf16[16,96,128]{2,1,0:T(8,128)(2,1)} %bitcast.104, bf16[48,256,128]{2,1,0:T(8,128)(2,1)} %bitcast.105, bf16[48,256,128]{2,1,0:T(8,128)(2,1)} %bitcast.106), custom_call_target="tpu_custom_call" | custom-call | tf_op jit(solution)/shard_map/pallas_call | solution.py:606
  164.4 0.8 reshape.255
  165.2 0.8 reshape.256
  168.0 0.8 copy.77
  168.8 65.9 %shard_map.177 = (bf16[4,768,256]{2,1,0:T(8,128)(2,1)}, f32[32,256]{1,0:T(8,128)}) custom-call(f32[8]{0:T(128)} %reshape.247.hc_in, f32[32]{0:T(128)} %reshape.248.hc_mix, f32[8]{0:T(128)} %reshape.249.hc_out, s32[16]{0:T(128)} %accepted.1, bf16[768,256]{1,0:T(8,128)(2,1)} %bitcast.111, bf16[4,768,256]{2,1,0:T(8,128)(2,1)} %get-tuple-element.32.streams, ...), custom_call_target="tpu_custom_call" | custom-call | tf_op jit(solution)/shard_map/pallas_call | solution.py:1008
  234.8 1.4 copy-done.1
  236.2 0.8 copy-done.2
  237.0 30.8 %shard_map.178 = bf16[512,393]{1,0:T(8,128)(2,1)S(1)} custom-call(f32[32,256]{1,0:T(8,128)S(1)} %copy-done.2, bf16[2,2048,256]{2,1,0:T(8,128)(2,1)S(1)} %copy-done, bf16[393,2048]{1,0:T(8,128)(2,1)S(1)} %bitcast.101), custom_call_target="tpu_custom_call" | custom-call | tf_op jit(solution)/shard_map/pallas_call | solution.py:1213
  267.8 1.0 reshape.258
  268.8 5.9 %all-to-all-start = ((bf16[256,2,393]{2,1,0:T(2,128)(2,1)}), bf16[256,2,393]{2,1,0:T(2,128)(2,1)S(1)}, u32[]{:S(2)}, u32[]{:S(2)}) async-start(bf16[256,2,393]{2,1,0:T(2,128)(2,1)} %reshape.258), calls=%async_computation | async-start | bytes 1048576 | tf_op jit(solution)/shard_map/all_to_all | solution.py:1336
  274.7 3.8 %copy.62 = bf16[768,4,256]{2,1,0:T(4,128)(2,1)} copy(bf16[768,4,256]{2,0,1:T(8,128)(2,1)} %bitcast.109) | data formatting | bytes 3145728
  278.5 9.9 %all-to-all-done = bf16[256,2,393]{2,1,0:T(2,128)(2,1)S(1)} async-done(((bf16[256,2,393]{2,1,0:T(2,128)(2,1)}), bf16[256,2,393]{2,1,0:T(2,128)(2,1)S(1)}, u32[]{:S(2)}, u32[]{:S(2)}) %all-to-all-start) | async-done | bytes 402464 | tf_op jit(solution)/shard_map/all_to_all | solution.py:1336
  288.5 2.1 reshape.259
  (60 shorter events, 11.8 us)
Async XLA Ops:
  7.2 56.7 %all-gather.2.cloned.1.call-start = ((), (), s32[]{:S(2)}) async-start(), calls=%async_computation.1 | async-start | bytes 3538944 | tf_op jit(solution)/shard_map/all_gather | solution.py:1278
  11.6 18.7 %copy-start.9 = (f32[2,4]{1,0:T(2,128)S(1)}, f32[2,4]{1,0:T(2,128)}, u32[]{:S(2)}) copy-start(f32[2,4]{1,0:T(2,128)} %param.18) | copy-start | bytes 100
  30.9 9.4 %copy-start.4 = (bf16[2048,3,256]{2,0,1:T(8,128)(2,1)S(1)}, bf16[2048,3,256]{2,0,1:T(8,128)(2,1)}, u32[]{:S(2)}) copy-start(bf16[2048,3,256]{2,0,1:T(8,128)(2,1)} %param.21) | copy-start | bytes 9437188
  40.3 3.6 %copy-start.12 = (s32[16,48]{1,0:T(8,128)S(1)}, s32[16,48]{1,0:T(8,128)}, u32[]{:S(2)}) copy-start(s32[16,48]{1,0:T(8,128)} %param.32) | copy-start | bytes 9220
  44.0 3.2 %copy-start.10 = (s32[16]{0:T(128)S(1)}, s32[16]{0:T(128)}, u32[]{:S(2)}) copy-start(s32[16]{0:T(128)} %param.31) | copy-start | bytes 196
  44.4 4.8 %copy-start.8 = (f32[2,4,4]{2,1,0:T(4,128)S(1)}, f32[2,4,4]{2,1,0:T(4,128)}, u32[]{:S(2)}) copy-start(f32[2,4,4]{2,1,0:T(4,128)} %param.19) | copy-start | bytes 388
  44.9 19.0 %copy-start.5 = (bf16[2048,3,256]{0,2,1:T(8,128)(2,1)S(1)}, bf16[2048,3,256]{0,2,1:T(8,128)(2,1)}, u32[]{:S(2)}) copy-start(bf16[2048,3,256]{0,2,1:T(8,128)(2,1)} %copy.48) | copy-start | bytes 9437188
  68.4 0.9 copy-start.6
  68.4 1.0 copy-start.7
  77.5 88.7 %copy-start.3 = (bf16[16,48,2,128]{3,1,2,0:T(8,128)(2,1)S(1)}, bf16[16,48,2,128]{3,1,2,0:T(8,128)(2,1)}, u32[]{:S(2)}) copy-start(bf16[16,48,2,128]{3,1,2,0:T(8,128)(2,1)} %fusion.9) | copy-start | bytes 1179652
  164.4 2.6 copy-start.11
  168.8 66.0 %copy-start = (bf16[2,2048,256]{2,1,0:T(8,128)(2,1)S(1)}, bf16[2,2048,256]{2,1,0:T(8,128)(2,1)}, u32[]{:S(2)}) copy-start(bf16[2,2048,256]{2,1,0:T(8,128)(2,1)} %weight_hbm.1) | copy-start | bytes 6291460
  234.8 1.4 copy-start.1
  236.2 0.8 copy-start.2
  268.8 19.5 %all-to-all-start = ((bf16[256,2,393]{2,1,0:T(2,128)(2,1)}), bf16[256,2,393]{2,1,0:T(2,128)(2,1)S(1)}, u32[]{:S(2)}, u32[]{:S(2)}) async-start(bf16[256,2,393]{2,1,0:T(2,128)(2,1)} %reshape.258), calls=%async_computation | async-start | bytes 1048576 | tf_op jit(solution)/shard_map/all_to_all | solution.py:1336
Sparse Core Ops, SparseCore 0:
  30.4 33.4 all-gather.1

commit v2 on v1

--- a/solution.py
+++ b/solution.py
@@ -9,72 +9,30 @@
 from jax.sharding import PartitionSpec as P
 
 NEG_FILL = -1e30
-PRECISE = lax.Precision.HIGHEST
-
-
-def layer_norm(values):
-    center = jnp.mean(values, axis=-1, keepdims=True)
-    square = jnp.mean(values * values, axis=-1, keepdims=True)
-    return (values - center) * lax.rsqrt(square - center * center + 1e-05)
-
-
-def normalize(values, sums, squares, width):
-    center = sums / width
-    return (values - center) * lax.rsqrt(squares / width - center * center + 1e-05)
 
 
 def ancestors(parents):
     length = parents.shape[1]
     places = jnp.arange(length, dtype=jnp.int32)
-    linked = (parents[:, :, None] == places[None, None, :]) | (places[:, None] == places[None, :])[
+    linked = (places[None, :, None] == parents[:, None, :]) | (places[:, None] == places[None, :])[
         None
     ]
-    reach = linked.astype(jnp.float32)
+    reach = linked.astype(jnp.bfloat16)
     for repeat in range(max(1, (length - 1).bit_length())):
-        reach = jnp.minimum(jnp.einsum("jik,jkl->jil", reach, reach, precision=PRECISE), 1.0)
+        counts = jnp.einsum("jki,jil->jkl", reach, reach, preferred_element_type=jnp.float32)
+        reach = jnp.minimum(counts, 1.0).astype(jnp.bfloat16)
     return reach
 
 
-def rotate(values, positions):
-    half = values.shape[-1] // 2
+def turns(positions, head_dim):
+    half = head_dim // 2
     freqs = jnp.exp(
-        jnp.arange(half, dtype=jnp.float32) * (-2.0 * math.log(10000.0) / values.shape[-1])
+        jnp.arange(half, dtype=jnp.float32) * (-2.0 * math.log(10000.0) / head_dim)
     )
     angles = positions.astype(jnp.float32)[:, None] * freqs[None, :]
-    cosine = jnp.cos(angles)[:, None, :]
-    sine = jnp.sin(angles)[:, None, :]
-    first = values[..., :half]
-    second = values[..., half:]
-    return jnp.concatenate(
-        [first * cosine - second * sine, second * cosine + first * sine], axis=-1
-    )
-
-
-def blend(stream_vals, weights):
-    total = weights[0] * stream_vals[:, 0]
-    for index in range(1, stream_vals.shape[1]):
-        total = total + weights[index] * stream_vals[:, index]
-    return total
-
-
-def remix(stream_vals, mixing, out_scale, delta):
-    count = stream_vals.shape[1]
-    matrix = jnp.eye(count, dtype=jnp.float32) + mixing
-    rows = [
-        blend(stream_vals, matrix[:, target]) + out_scale[target] * delta for target in range(count)
-    ]
-    return jnp.stack(rows, axis=1)
-
-
-def stream_total(stream_vals):
-    total = stream_vals[:, 0]
-    for index in range(1, stream_vals.shape[1]):
-        total = total + stream_vals[:, index]
-    return total
-
-
-def fold_rows(weight, piece):
-    return jnp.dot(piece, weight, preferred_element_type=jnp.float32)
+    cosine = jnp.cos(angles)
+    sine = jnp.sin(angles)
+    return jnp.concatenate([cosine, cosine], axis=1), jnp.concatenate([-sine, sine], axis=1)
 
 
 MESH = pl.DeviceIdType.MESH
@@ -105,11 +63,14 @@
     table,
     last,
     q_ref,
+    key_ref,
+    value_ref,
+    mask_ref,
     k_hbm,
     v_hbm,
-    num_ref,
-    top_ref,
-    den_ref,
+    out_ref,
+    tree_acc,
+    tree_stat,
     q_all,
     k_buf,
     v_buf,
@@ -225,6 +186,29 @@
     seg_top[...] = jnp.full(seg_top.shape, NEG_FILL, jnp.float32)
     seg_den[...] = jnp.zeros(seg_den.shape, jnp.float32)
     seg_acc[slots] = jnp.zeros(seg_acc.shape[1:], seg_acc.dtype)
+    tree_stat[...] = jnp.zeros(tree_stat.shape, jnp.float32)
+
+    def tree_step(item, carry):
+        found = lax.dot_general(
+            key_ref[item],
+            q_ref[item],
+            (((1,), (1,)), ((), ())),
+            preferred_element_type=jnp.float32,
+        )
+        found = jnp.where(mask_ref[item].astype(jnp.float32) > 0.0, found, NEG_FILL)
+        top = jnp.max(found, axis=0, keepdims=True)
+        weight = jnp.exp(found - top)
+        tree_acc[item] = lax.dot_general(
+            weight.astype(jnp.bfloat16),
+            value_ref[item],
+            (((0,), (0,)), ((), ())),
+            preferred_element_type=jnp.float32,
+        )
+        tree_stat[0, item, :, 0:rows] = top
+        tree_stat[1, item, :, 0:rows] = jnp.sum(weight, axis=0, keepdims=True)
+        return carry
+
+    lax.fori_loop(0, 2 * block, tree_step, 0)
     for half in halves:
         lines[half, 0].wait_recv()
         line(half, 2, turn, at(first[half], -turn))
@@ -495,8 +479,6 @@
         p1 = at(first[half], 2)
         tail(half, 0, small.at[half, p1], small_s.at[half, p1], turn)
     lax.fori_loop(1, 2, piece_step, 0)
-    for half in halves:
-        p1 = at(first[half], -turn + 2 + 2)
     lax.fori_loop(2, 4, piece_step, 0)
     for half in halves:
         p1 = at(first[half], -turn)
@@ -522,17 +504,38 @@
         for index in (1, 2):
             for copy in tails[half, index]:
                 copy.wait_recv()
+        tree = [
+            jnp.concatenate(
+                [tree_stat[kind, half * block + item] for item in range(block)], axis=0
+            )
+            for kind in (0, 1)
+        ]
         top, den, weights = weigh(
-            [small_s[half, p1, 0], hop_s[half, 1, 0], hop_s[half, 2, 0]],
-            [small_s[half, p1, 1], hop_s[half, 1, 1], hop_s[half, 2, 1]],
-        )
-        top_ref[half * block : (half + 1) * block] = top
-        den_ref[half * block : (half + 1) * block] = den
+            [small_s[half, p1, 0], hop_s[half, 1, 0], hop_s[half, 2, 0], tree[0]],
+            [small_s[half, p1, 1], hop_s[half, 1, 1], hop_s[half, 2, 1], tree[1]],
+        )
+        lane = lax.broadcasted_iota(jnp.int32, den.shape, 1)
+        inverse = 1.0 / jnp.where(lane < rows, den, 1.0)
 
         def put(item, value, half=half):
-            num_ref[half * block + item] = value
-
-        combine(put, [small.at[half, p1], hop.at[half, 1], hop.at[half, 2]], weights)
+            start = (half * block + item) * half_rows
+            value = value.astype(out_ref.dtype)
+            width = value.shape[1]
+            for head in (0, 1):
+                out_ref[start : start + half_rows, head * width : (head + 1) * width] = value[
+                    head * half_rows : (head + 1) * half_rows
+                ]
+
+        combine(
+            put,
+            [
+                small.at[half, p1],
+                hop.at[half, 1],
+                hop.at[half, 2],
+                tree_acc.at[pl.ds(half * block, block)],
+            ],
+            [weight * inverse for weight in weights],
+        )
     for copy in sends:
         copy.wait_send()
     for half in halves:
@@ -540,7 +543,9 @@
             join_copy(half, order).wait_send()
 
 
-def cache_attention(queries, k_pages, v_pages, page_owner, page_fill):
+def cache_attention(
+    queries, keys_new, values_new, tree_mask, k_pages, v_pages, page_owner, page_fill
+):
     req_local, rows, head_dim = queries.shape
     slots, keys = k_pages.shape[0], k_pages.shape[1] * k_pages.shape[2]
     devices = lax.axis_size("req")
@@ -569,6 +574,8 @@
     unit = (2, side, block, rows, head_dim)
     dma = pltpu.SemaphoreType.DMA
     scratch = [
+        pltpu.VMEM((req_local, rows, head_dim), f32),
+        pltpu.VMEM((2, req_local, 1, 128), f32),
         pltpu.VMEM((requests, rows, head_dim), bf16),
         pltpu.VMEM((slots, keys, head_dim), bf16),
         pltpu.VMEM((slots, keys, head_dim), bf16),
@@ -605,13 +612,9 @@
     anywhere = pl.BlockSpec(memory_space=pl.ANY)
     return pl.pallas_call(
         functools.partial(cache_kernel, side),
-        out_shape=(
-            jax.ShapeDtypeStruct((req_local, rows, head_dim), f32),
-            jax.ShapeDtypeStruct((req_local, 128), f32),
-            jax.ShapeDtypeStruct((req_local, 128), f32),
-        ),
-        in_specs=[smem, smem, vmem, anywhere, anywhere],
-        out_specs=(vmem, vmem, vmem),
+        out_shape=jax.ShapeDtypeStruct((req_local * rows // 2, 2 * head_dim), bf16),
+        in_specs=[smem, smem] + [vmem] * 4 + [anywhere, anywhere],
+        out_specs=vmem,
         scratch_shapes=scratch,
         compiler_params=pltpu.CompilerParams(
             collective_id=0, has_side_effects=True, vmem_limit_bytes=56 << 20
@@ -620,6 +623,9 @@
         table,
         last,
         queries,
+        keys_new,
+        values_new,
+        tree_mask,
         k_pages.reshape(slots, keys, head_dim),
         v_pages.reshape(slots, keys, head_dim),
     )
@@ -1233,6 +1239,220 @@
     )(final_rows, draft_weight, jnp.transpose(lm_head))
 
 
+def front_kernel(
+    chips,
+    chunks,
+    hc_in,
+    streams,
+    cosine,
+    sine,
+    weight_hbm,
+    query_ref,
+    key_ref,
+    value_ref,
+    weight_buf,
+    mixed_buf,
+    stat_all,
+    columns,
+    normed,
+    gathered,
+    load_sem,
+    own_sem,
+    stat_send,
+    stat_recv,
+    copy_send,
+    copy_recv,
+    pass_send,
+    pass_recv,
+):
+    count, tokens, feature = streams.shape
+    size = tokens // chunks
+    group = 2 * chips
+    width = group * feature
+    requests, rows, head_dim = query_ref.shape
+    heads = feature // head_dim
+    tree = rows // heads
+    me = lax.axis_index("head")
+    chip = me // 2
+    core = lax.rem(me, 2)
+    turn = 1 - 2 * core
+    sibling = chip * 2 + 1 - core
+
+    def peer(delta):
+        return lax.rem(chip + chips + delta, chips) * 2 + core
+
+    def send_to(source, target, send_sem, recv_sem, head):
+        return pltpu.make_async_remote_copy(
+            src_ref=source,
+            dst_ref=target,
+            send_sem=send_sem,
+            recv_sem=recv_sem,
+            device_id={"head": head},
+            device_id_type=MESH,
+        )
+
+    load = pltpu.make_async_copy(weight_hbm, weight_buf, load_sem)
+    load.start()
+    barrier = pltpu.get_barrier_semaphore()
+    for step in range(1, group):
+        pl.semaphore_signal(
+            barrier, inc=1, device_id={"head": lax.rem(me + step, group)}, device_id_type=MESH
+        )
+    block = 32
+    for t in range(chunks):
+
+        def mix(index, carry, t=t):
+            here = pl.ds(t * size + index * block, block)
+            mixed = None
+            for s in range(count):
+                term = hc_in[s] * streams[s, here].astype(jnp.float32)
+                mixed = term if mixed is None else mixed + term
+            mixed_buf[here] = mixed
+            return carry
+
+        lax.fori_loop(0, size // block, mix, 0)
+        mixed = mixed_buf[t * size : (t + 1) * size]
+        stat_all[t, me, 0:1] = transpose_sum(mixed)
+        stat_all[t, me, 1:2] = transpose_sum(mixed * mixed)
+        stat_all[t, me, 2:8] = jnp.zeros((6, size), jnp.float32)
+    pl.semaphore_wait(barrier, group - 1)
+
+    sends = []
+    waits = {}
+
+    def go(copy):
+        copy.start()
+        sends.append(copy)
+        return copy
+
+    def chunk_rows(t):
+        return pl.ds(t * size, size)
+
+    def lanes(head):
+        return pl.ds(pl.multiple_of(head * feature, feature), feature)
+
+    for t in range(chunks):
+        for step in range(1, group):
+            waits["stat", t, step] = go(
+                send_to(stat_all.at[t, me], stat_all.at[t, me], stat_send.at[t, step],
+                        stat_recv.at[t, step], lax.rem(me + step, group)))
+
+    def normalized(t):
+        for step in range(1, group):
+            waits["stat", t, step].wait_recv()
+        total = stat_all[t, 0]
+        for index in range(1, group):
+            total = total + stat_all[t, index]
+        center = total[0:1] / width
+        scale = lax.rsqrt(total[1:2] / width - center * center + 1e-05)
+        row = lax.broadcasted_iota(jnp.int32, total.shape, 0)
+        packed = jnp.where(row == 0, center, jnp.where(row == 1, scale, 0.0))
+        columns[t] = jnp.transpose(packed)
+
+        def step(index, carry):
+            inside = pl.ds(index * block, block)
+            here = pl.ds(t * size + index * block, block)
+            column = columns[t, inside]
+            value = (mixed_buf[here] - column[:, 0:1]) * column[:, 1:2]
+            normed[here] = value.astype(normed.dtype)
+            return carry
+
+        lax.fori_loop(0, size // block, step, 0)
+        mine = normed.at[chunk_rows(t)]
+        view = gathered.at[chunk_rows(t), lanes(me)]
+        waits["fwd", t] = go(send_to(mine, view, pass_send.at[t, 0], pass_recv.at[t, 0], peer(turn)))
+        waits["bwd", t] = go(send_to(mine, view, pass_send.at[t, 1], pass_recv.at[t, 1], peer(-turn)))
+        waits["own", t] = go(send_to(mine, view, copy_send.at[t, 0], copy_recv.at[t, 0], sibling))
+        local = pltpu.make_async_copy(mine, view, own_sem.at[t])
+        local.start()
+        waits["local", t] = local
+
+    def hand_over(t, index, delta):
+        view = gathered.at[chunk_rows(t), lanes(peer(delta))]
+        waits["copy", t, index] = go(
+            send_to(view, view, copy_send.at[t, index], copy_recv.at[t, index], sibling))
+
+    def pass_on(t):
+        waits["fwd", t].wait_recv()
+        view = gathered.at[chunk_rows(t), lanes(peer(-turn))]
+        waits["opp", t] = go(send_to(view, view, pass_send.at[t, 2], pass_recv.at[t, 2], peer(turn)))
+        hand_over(t, 1, -turn)
+        waits["bwd", t].wait_recv()
+        hand_over(t, 2, turn)
+
+    def pass_last(t):
+        waits["opp", t].wait_recv()
+        hand_over(t, 3, 2)
+
+    def project(t):
+        if t == 0:
+            load.wait()
+        waits["own", t].wait_recv()
+        waits["local", t].wait()
+        for index in (1, 2, 3):
+            waits["copy", t, index].wait_recv()
+        here = slice(t * size, (t + 1) * size)
+        for kind, target in enumerate((query_ref, key_ref, value_ref)):
+            product = jnp.dot(gathered[here], weight_buf[kind], preferred_element_type=jnp.float32)
+            for head in range(heads):
+                value = product[:, head * head_dim : (head + 1) * head_dim]
+                if kind < 2:
+                    turned = pltpu.roll(value, head_dim // 2, 1)
+                    value = value * cosine[here] + turned * sine[here]
+                if kind == 0:
+                    value = value * head_dim ** (-0.5)
+                value = value.astype(target.dtype)
+                for item in range(size // tree):
+                    target[t * (size // tree) + item, head * tree : (head + 1) * tree] = value[
+                        item * tree : (item + 1) * tree
+                    ]
+
+    phases = (normalized, pass_on, pass_last, project)
+    for step in range(len(phases) + chunks - 1):
+        for t in range(chunks):
+            if 0 <= step - t < len(phases):
+                phases[step - t](t)
+    for copy in sends:
+        copy.wait_send()
+
+
+def front(streams, hc_in, qkv, cosine, sine, requests, heads):
+    count, tokens, feature = streams.shape
+    group = lax.axis_size("head")
+    width = qkv.shape[1]
+    chunks = 2
+    size = tokens // chunks
+    rows = heads * (tokens // requests)
+    head_dim = feature // heads
+    bf16, f32 = jnp.bfloat16, jnp.float32
+    dma = pltpu.SemaphoreType.DMA
+    vmem = pl.BlockSpec(memory_space=pltpu.VMEM)
+    smem = pl.BlockSpec(memory_space=pltpu.SMEM)
+    anywhere = pl.BlockSpec(memory_space=pl.ANY)
+    return pl.pallas_call(
+        functools.partial(front_kernel, group // 2, chunks),
+        out_shape=(jax.ShapeDtypeStruct((requests, rows, head_dim), bf16),) * 3,
+        in_specs=[smem, vmem, vmem, vmem, anywhere],
+        out_specs=(vmem,) * 3,
+        scratch_shapes=[
+            pltpu.VMEM(qkv.shape, bf16),
+            pltpu.VMEM((tokens, feature), f32),
+            pltpu.VMEM((chunks, group, 8, size), f32),
+            pltpu.VMEM((chunks, size, 8), f32),
+            pltpu.VMEM((tokens, feature), bf16),
+            pltpu.VMEM((tokens, width), bf16),
+            dma,
+            dma((chunks,)),
+            dma((chunks, group)), dma((chunks, group)),
+            dma((chunks, 4)), dma((chunks, 4)),
+            dma((chunks, 3)), dma((chunks, 3)),
+        ],
+        compiler_params=pltpu.CompilerParams(
+            collective_id=3, has_side_effects=True, vmem_limit_bytes=40 << 20
+        ),
+    )(hc_in.reshape(-1), streams, cosine, sine, qkv)
+
+
 def on_device(
     streams,
     hc_in,
@@ -1253,74 +1473,37 @@
     accepted_index,
 ):
     tokens_local = streams.shape[0]
-    feature_local = streams.shape[2]
-    width = qkv_weight.shape[0]
     req_local = cache_len.shape[0]
     tree_size = tree_parent.shape[1]
-    slot_count = k_pages.shape[0]
-    page_size = k_pages.shape[1]
     heads_local = k_pages.shape[2]
     head_dim = k_pages.shape[3]
     draft_count = draft_weight.shape[0]
     all_requests = req_local * lax.axis_size("req")
     reach = ancestors(tree_parent)
-    depth = (jnp.sum(reach, axis=2) - 1.0).astype(jnp.int32)
+    depth = (jnp.sum(reach.astype(jnp.float32), axis=1) - 1.0).astype(jnp.int32)
     positions = (cache_len[:, None] + depth).reshape(tokens_local)
-    stream_vals = streams.astype(jnp.float32)
-    mixed_in = blend(stream_vals, hc_in[0])
-    stat_sum, stat_square = lax.psum(
-        (jnp.sum(mixed_in, axis=1), jnp.sum(mixed_in * mixed_in, axis=1)), "head"
+    cosine, sine = turns(positions, head_dim)
+    same_head = jnp.eye(heads_local, dtype=jnp.bfloat16)
+    tree_mask = (same_head[None, :, None, :, None] * reach[:, None, :, None, :]).reshape(
+        req_local, heads_local * tree_size, heads_local * tree_size
     )
-    normed = normalize(mixed_in, stat_sum[:, None], stat_square[:, None], width).astype(
-        jnp.bfloat16
+    gate_up = jnp.transpose(up_gate, (1, 0, 2))
+    by_stream = jnp.transpose(streams, (1, 0, 2))
+    queries, keys_new, values_new = front(
+        by_stream,
+        hc_in,
+        jnp.transpose(qkv_weight, (1, 0, 2)),
+        cosine,
+        sine,
+        req_local,
+        heads_local,
     )
-    qkv_flat = qkv_weight.reshape(width, -1)
-    normed_full = lax.all_gather(normed, "head", axis=1, tiled=True)
-    gate_up = jnp.transpose(up_gate, (1, 0, 2))
-    normed_full, gate_up = lax.optimization_barrier((normed_full, gate_up))
-    projected = fold_rows(qkv_flat, normed_full)
-    projected = projected.reshape(tokens_local, 3, heads_local, head_dim)
-    queries = (rotate(projected[:, 0], positions) * head_dim ** (-0.5)).astype(jnp.bfloat16)
-    keys_new = rotate(projected[:, 1], positions).astype(jnp.bfloat16)
-    values_new = projected[:, 2].astype(jnp.bfloat16)
-    query_rows = (
-        queries.reshape(req_local, tree_size, heads_local, head_dim)
-        .transpose(0, 2, 1, 3)
-        .reshape(req_local, heads_local * tree_size, head_dim)
-    )
-    own_sum, own_top, own_den = cache_attention(
-        query_rows, k_pages, v_pages, page_owner, page_fill
-    )
-    own_sum = own_sum.reshape(req_local, heads_local, tree_size, head_dim).transpose(0, 2, 1, 3)
-    used = heads_local * tree_size
-    own_top = own_top[:, :used].reshape(req_local, heads_local, tree_size).transpose(0, 2, 1)
-    own_den = own_den[:, :used].reshape(req_local, heads_local, tree_size).transpose(0, 2, 1)
-    query_own = queries.reshape(req_local, tree_size, heads_local, head_dim)
-    keys_own = keys_new.reshape(req_local, tree_size, heads_local, head_dim)
-    values_own = values_new.reshape(req_local, tree_size, heads_local, head_dim)
-    tree_scores = jnp.einsum(
-        "jqhd,jkhd->jqhk", query_own, keys_own, preferred_element_type=jnp.float32
-    )
-    tree_mask = (reach > 0)[:, :, None, :]
-    tree_scores = jnp.where(tree_mask, tree_scores, NEG_FILL)
-    top = jnp.maximum(own_top, jnp.max(tree_scores, axis=3))
-    carried = jnp.exp(own_top - top)
-    tree_weights = jnp.where(tree_mask, jnp.exp(tree_scores - top[..., None]), 0.0)
-    denominator = own_den * carried + jnp.sum(tree_weights, axis=3)
-    numerator = own_sum * carried[..., None] + jnp.einsum(
-        "jqhk,jkhd->jqhd",
-        tree_weights.astype(jnp.bfloat16),
-        values_own,
-        preferred_element_type=jnp.float32,
-    )
-    attended = (
-        (numerator / denominator[..., None])
-        .astype(jnp.bfloat16)
-        .reshape(tokens_local, heads_local * head_dim)
+    attended = cache_attention(
+        queries, keys_new, values_new, tree_mask, k_pages, v_pages, page_owner, page_fill
     )
     fresh, final_local = layer(
         attended,
-        jnp.transpose(streams, (1, 0, 2)),
+        by_stream,
         hc_in,
         hc_mix,
         hc_out,

time: 302 us -> 270 us (0.89); the launches traced: 298 us -> 269 us
  Pallas kernels: 184 us -> 219 us
  blocking collectives: 14.7 us -> 0 us
  between operations: 14.6 us -> 0.85 us
  local copies, waits for them, and re-layouts: 37.6 us -> 26.2 us
  waiting for transfers between devices: 18.9 us -> 9.91 us
  other arithmetic: 13.6 us -> 5.47 us
  matrix products: 8.78 us -> 2.44 us
    pallas_call x1 -> x2, Pallas kernels: 86.9 us -> 122 us  [the longest x1 87.2 us: cache_attention(): pl.pallas_call(functools.partial(cache_kernel, side), out_shape=jax.Shape...]
    psum x1 -> x0, blocking collectives: 14.7 us -> none  [on_device(): lax.psum((jnp.sum(mixed_in, axis=1), jnp.sum(mixed_in * mixed_in, axis=1)...]
    all_gather x1 -> x0, waiting for transfers between devices: 8.97 us -> none  [on_device(): normed_full = lax.all_gather(normed, 'head', axis=1, tiled=True)]
    dot_general x9 -> x3, matrix products: 8.78 us -> 2.44 us  [ancestors(): jnp.einsum('jki,jil->jkl', reach, reach, preferred_element_type=jnp.float32)]
    concatenate x8 -> x0, local copies, waits for them, and re-layouts: 6.09 us -> none  [rotate(): jnp.concatenate([first * cosine - second * sine, second * cosine + first...]
    reduce_sum x3 -> x0, other arithmetic: 3.15 us -> none  [the longest x1 2.72 us: on_device(): jnp.sum(mixed_in, axis=1)]
    unnamed x30 -> x23, local copies, waits for them, and re-layouts: 20.7 us -> 18.4 us
  transfers between devices with their start and end apart: 2 -> 1, of which waited for: 2 -> 1; matrix products, arithmetic and copies ran while one was open for 9% -> 1% of each run, Pallas kernels for 0% -> 0%
where the time goes in v2:
time: 270 us; the launch traced here: 269 us
  Pallas kernels  219 us (81%)
  local copies, waits for them, and re-layouts  26.2 us (10%)
  waiting for transfers between devices  9.91 us (4%)
  starting transfers between devices  5.5 us (2%)
  other arithmetic  5.47 us (2%)
    pallas_call x1, Pallas kernels, cache_attention(): pl.pallas_call(functools.partial(cache_kernel, side), out_shape=jax.Shape...  87.2 us
    pallas_call x1, Pallas kernels, layer(): pl.pallas_call(functools.partial(layer_kernel, chips, chunks), out_shape=...  66.3 us
    pallas_call x1, Pallas kernels, front(): pl.pallas_call(functools.partial(front_kernel, group // 2, chunks), out_s...  34.4 us
    pallas_call x1, Pallas kernels, draft_logits(): pl.pallas_call(functools.partial(draft_kernel, group // 2), out_shape=jax...  31.1 us
    unnamed x23, local copies, waits for them, and re-layouts  18.4 us
    all_to_all x1, waiting for transfers between devices, on_device(): lax.all_to_all(logits_local, ('req', 'head'), split_axis=0, concat_axis=2...  9.91 us
    all_to_all x1, starting transfers between devices, on_device(): lax.all_to_all(logits_local, ('req', 'head'), split_axis=0, concat_axis=2...  5.5 us
  transfers between devices with their start and end apart: 1, of which 1 were waited for; matrix products, arithmetic and copies ran while one was open for 1% of the time, Pallas kernels for 0%

profile of v2, /device:TPU:1, one launch (start us, length us, event | category | flops | bytes accessed | tf_op | source)
XLA Modules:
  0.0 269.3 jit_solution(10779176808674805174)
XLA Ops:
  0.7 0.9 reshape.150.hc_in
  1.6 1.3 reshape.151.hc_mix
  2.9 1.2 reshape.152.hc_out
  4.2 0.7 compare_select_fusion.5
  4.8 0.2 convert_reduce_fusion.3
  5.0 0.6 select_reduce_fusion.table
  5.8 1.4 fusion.1
  7.3 0.5 fusion.3
  7.8 0.5 convert_reduce_fusion
  8.3 0.7 add_convert_fusion
  9.1 0.5 mul.96
  9.6 0.3 mul.97
  10.0 0.2 copy.35
  10.2 9.8 %copy.34 = bf16[2048,2,1024]{2,0,1:T(8,128)(2,1)} copy(bf16[2048,2,1024]{2,1,0:T(2,128)(2,1)} %param.23) | data formatting | bytes 16777216 | tf_op args[6]
  20.1 0.6 compare_select_fusion.6.last
  20.7 0.8 broadcast_multiply_fusion.mask_ref
  21.5 1.4 fusion.16
  23.0 0.3 pad_maximum_fusion
  23.3 34.4 %shard_map.176 = (bf16[16,96,128]{2,1,0:T(8,128)(2,1)S(1)}, bf16[16,96,128]{2,1,0:T(8,128)(2,1)S(1)}, bf16[16,96,128]{2,1,0:T(8,128)(2,1)S(1)}) custom-call(f32[8]{0:T(128)S(1)} %reshape.150.hc_in, bf16[4,768,256]{2,1,0:T(8,128)(2,1)S(1)} %bitcast.22, f32[768,128]{1,0:T(8,128)S(1)} %get-tuple-element.27.cosine, f32[768,128]{1,0:T(8,128)S(1)} %get-tuple-element.28.sine, ...), custom_call_target="tpu_custom_call" | custom-call | tf_op jit(solution)/shard_map/pallas_call | solution.py:1432
  57.7 0.7 copy-done.4
  58.4 0.8 copy-done.5
  59.2 0.8 copy-done.6
  60.0 87.2 %shard_map.177.attended = bf16[768,256]{1,0:T(8,128)(2,1)} custom-call(s32[48]{0:T(128)} %select_reduce_fusion.table, s32[256]{0:T(256)} %compare_select_fusion.6.last, bf16[16,96,128]{2,1,0:T(8,128)(2,1)} %copy-done.4, bf16[16,96,128]{2,1,0:T(8,128)(2,1)} %copy-done.5, bf16[16,96,128]{2,1,0:T(8,128)(2,1)} %copy-done.6, ...), custom_call_target="tpu_custom_call" | custom-call | tf_op jit(solution)/shard_map/pallas_call | solution.py:613
  147.3 66.3 %shard_map.178 = (bf16[4,768,256]{2,1,0:T(8,128)(2,1)}, f32[32,256]{1,0:T(8,128)}) custom-call(f32[8]{0:T(128)} %copy-done.8, f32[32]{0:T(128)} %reshape.151.hc_mix, f32[8]{0:T(128)} %reshape.152.hc_out, s32[16]{0:T(128)} %accepted.1, bf16[768,256]{1,0:T(8,128)(2,1)} %shard_map.177.attended, bf16[4,768,256]{2,1,0:T(8,128)(2,1)} %bitcast.23, ...), custom_call_target="tpu_custom_call" | custom-call | tf_op jit(solution)/shard_map/pallas_call | solution.py:1014
  213.6 1.4 copy-done.3
  215.0 0.8 copy-done.7
  215.8 31.1 %shard_map.179 = bf16[512,393]{1,0:T(8,128)(2,1)S(1)} custom-call(f32[32,256]{1,0:T(8,128)S(1)} %copy-done.7, bf16[2,2048,256]{2,1,0:T(8,128)(2,1)S(1)} %copy-done.2, bf16[393,2048]{1,0:T(8,128)(2,1)S(1)} %bitcast.25), custom_call_target="tpu_custom_call" | custom-call | tf_op jit(solution)/shard_map/pallas_call | solution.py:1219
  246.9 1.0 reshape.155
  247.9 5.5 %all-to-all-start = ((bf16[256,2,393]{2,1,0:T(2,128)(2,1)}), bf16[256,2,393]{2,1,0:T(2,128)(2,1)S(1)}, u32[]{:S(2)}, u32[]{:S(2)}) async-start(bf16[256,2,393]{2,1,0:T(2,128)(2,1)} %reshape.155), calls=%async_computation | async-start | bytes 1048576 | tf_op jit(solution)/shard_map/all_to_all | solution.py:1519
  253.4 3.8 %copy.30 = bf16[768,4,256]{2,1,0:T(4,128)(2,1)} copy(bf16[768,4,256]{2,0,1:T(8,128)(2,1)} %bitcast.31) | data formatting | bytes 3145728
  257.2 9.9 %all-to-all-done = bf16[256,2,393]{2,1,0:T(2,128)(2,1)S(1)} async-done(((bf16[256,2,393]{2,1,0:T(2,128)(2,1)}), bf16[256,2,393]{2,1,0:T(2,128)(2,1)S(1)}, u32[]{:S(2)}, u32[]{:S(2)}) %all-to-all-start) | async-done | bytes 402464 | tf_op jit(solution)/shard_map/all_to_all | solution.py:1519
  267.2 2.1 reshape.156
  (24 shorter events, 0.6 us)
Async XLA Ops:
  0.6 9.4 %copy-start.9 = (bf16[768,4,256]{2,1,0:T(4,128)(2,1)S(1)}, bf16[768,4,256]{2,1,0:T(4,128)(2,1)}, u32[]{:S(2)}) copy-start(bf16[768,4,256]{2,1,0:T(4,128)(2,1)} %param.17) | copy-start | bytes 4718596
  1.6 21.7 %copy-start.8 = (f32[8]{0:T(128)}, f32[8]{0:T(128)S(1)}, u32[]{:S(2)}) copy-start(f32[8]{0:T(128)S(1)} %reshape.150.hc_in) | copy-start | bytes 100
  10.2 13.1 %copy-start = (bf16[768,4,256]{2,0,1:T(8,128)(2,1)}, bf16[768,4,256]{2,0,1:T(8,128)(2,1)S(1)}, u32[]{:S(2)}) copy-start(bf16[768,4,256]{2,0,1:T(8,128)(2,1)S(1)} %copy.35) | copy-start | bytes 4718596
  20.1 3.2 %copy-start.1 = (bf16[2048,3,256]{2,0,1:T(8,128)(2,1)S(1)}, bf16[2048,3,256]{2,0,1:T(8,128)(2,1)}, u32[]{:S(2)}) copy-start(bf16[2048,3,256]{2,0,1:T(8,128)(2,1)} %param.21) | copy-start | bytes 9437188
  57.7 0.7 copy-start.4
  58.4 0.8 copy-start.5
  59.2 0.8 copy-start.6
  147.2 66.3 %copy-start.2 = (bf16[2,2048,256]{2,1,0:T(8,128)(2,1)S(1)}, bf16[2,2048,256]{2,1,0:T(8,128)(2,1)}, u32[]{:S(2)}) copy-start(bf16[2,2048,256]{2,1,0:T(8,128)(2,1)} %weight_hbm.1) | copy-start | bytes 6291460
  213.6 1.4 copy-start.3
  215.0 0.8 copy-start.7
  247.9 19.2 %all-to-all-start = ((bf16[256,2,393]{2,1,0:T(2,128)(2,1)}), bf16[256,2,393]{2,1,0:T(2,128)(2,1)S(1)}, u32[]{:S(2)}, u32[]{:S(2)}) async-start(bf16[256,2,393]{2,1,0:T(2,128)(2,1)} %reshape.155), calls=%async_computation | async-start | bytes 1048576 | tf_op jit(solution)/shard_map/all_to_all | solution.py:1519

commit v3 on v1

--- a/solution.py
+++ b/solution.py
@@ -9,72 +9,30 @@
 from jax.sharding import PartitionSpec as P
 
 NEG_FILL = -1e30
-PRECISE = lax.Precision.HIGHEST
-
-
-def layer_norm(values):
-    center = jnp.mean(values, axis=-1, keepdims=True)
-    square = jnp.mean(values * values, axis=-1, keepdims=True)
-    return (values - center) * lax.rsqrt(square - center * center + 1e-05)
-
-
-def normalize(values, sums, squares, width):
-    center = sums / width
-    return (values - center) * lax.rsqrt(squares / width - center * center + 1e-05)
 
 
 def ancestors(parents):
     length = parents.shape[1]
     places = jnp.arange(length, dtype=jnp.int32)
-    linked = (parents[:, :, None] == places[None, None, :]) | (places[:, None] == places[None, :])[
+    linked = (places[None, :, None] == parents[:, None, :]) | (places[:, None] == places[None, :])[
         None
     ]
-    reach = linked.astype(jnp.float32)
+    reach = linked.astype(jnp.bfloat16)
     for repeat in range(max(1, (length - 1).bit_length())):
-        reach = jnp.minimum(jnp.einsum("jik,jkl->jil", reach, reach, precision=PRECISE), 1.0)
+        counts = jnp.einsum("jki,jil->jkl", reach, reach, preferred_element_type=jnp.float32)
+        reach = jnp.minimum(counts, 1.0).astype(jnp.bfloat16)
     return reach
 
 
-def rotate(values, positions):
-    half = values.shape[-1] // 2
+def turns(positions, head_dim):
+    half = head_dim // 2
     freqs = jnp.exp(
-        jnp.arange(half, dtype=jnp.float32) * (-2.0 * math.log(10000.0) / values.shape[-1])
+        jnp.arange(half, dtype=jnp.float32) * (-2.0 * math.log(10000.0) / head_dim)
     )
     angles = positions.astype(jnp.float32)[:, None] * freqs[None, :]
-    cosine = jnp.cos(angles)[:, None, :]
-    sine = jnp.sin(angles)[:, None, :]
-    first = values[..., :half]
-    second = values[..., half:]
-    return jnp.concatenate(
-        [first * cosine - second * sine, second * cosine + first * sine], axis=-1
-    )
-
-
-def blend(stream_vals, weights):
-    total = weights[0] * stream_vals[:, 0]
-    for index in range(1, stream_vals.shape[1]):
-        total = total + weights[index] * stream_vals[:, index]
-    return total
-
-
-def remix(stream_vals, mixing, out_scale, delta):
-    count = stream_vals.shape[1]
-    matrix = jnp.eye(count, dtype=jnp.float32) + mixing
-    rows = [
-        blend(stream_vals, matrix[:, target]) + out_scale[target] * delta for target in range(count)
-    ]
-    return jnp.stack(rows, axis=1)
-
-
-def stream_total(stream_vals):
-    total = stream_vals[:, 0]
-    for index in range(1, stream_vals.shape[1]):
-        total = total + stream_vals[:, index]
-    return total
-
-
-def fold_rows(weight, piece):
-    return jnp.dot(piece, weight, preferred_element_type=jnp.float32)
+    cosine = jnp.cos(angles)
+    sine = jnp.sin(angles)
+    return jnp.concatenate([cosine, cosine], axis=1), jnp.concatenate([-sine, sine], axis=1)
 
 
 MESH = pl.DeviceIdType.MESH
@@ -102,14 +60,43 @@
 
 def cache_kernel(
     side,
+    chips,
     table,
     last,
-    q_ref,
+    hc_in,
+    streams,
+    cosine,
+    sine,
+    mask_ref,
+    weight_hbm,
+    up_hbm,
     k_hbm,
     v_hbm,
-    num_ref,
-    top_ref,
-    den_ref,
+    out_ref,
+    gate_ref,
+    q_ref,
+    key_ref,
+    value_ref,
+    weight_buf,
+    mixed_buf,
+    stat_all,
+    columns,
+    normed,
+    gathered,
+    up_in,
+    up_out,
+    front_sem,
+    own_sem,
+    front_send,
+    front_recv,
+    copy_send,
+    copy_recv,
+    pass_send,
+    pass_recv,
+    up_in_sem,
+    up_out_sem,
+    tree_acc,
+    tree_stat,
     q_all,
     k_buf,
     v_buf,
@@ -174,15 +161,75 @@
         pltpu.make_async_copy(k_hbm, k_buf, load_sem.at[0]),
         pltpu.make_async_copy(v_hbm, v_buf, load_sem.at[1]),
     ]
-    for load in loads:
-        load.start()
+    weight_load = pltpu.make_async_copy(weight_hbm, weight_buf, front_sem)
+    weight_load.start()
     barrier = pltpu.get_barrier_semaphore()
     for axis in (0, 1):
         for delta in (1, -1):
             pl.semaphore_signal(
                 barrier, inc=1, device_id={"req": shifted(axis, delta)}, device_id_type=MESH
             )
-    pl.semaphore_wait(barrier, 4)
+    head_index = lax.axis_index("head")
+    for step in range(1, 2 * chips):
+        pl.semaphore_signal(
+            barrier,
+            inc=1,
+            device_id={"head": lax.rem(head_index + step, 2 * chips)},
+            device_id_type=MESH,
+        )
+
+    def enter():
+        pl.semaphore_wait(barrier, 4 + 2 * chips - 1)
+
+    pieces = gate_ref.shape[1] // up_out.shape[2]
+    span = up_out.shape[2]
+    tall = up_in.shape[1]
+
+    def up_load(c):
+        return pltpu.make_async_copy(
+            up_hbm.at[pl.ds(c * tall, tall)], up_in.at[c % 2], up_in_sem.at[c]
+        )
+
+    def up_store(c):
+        return pltpu.make_async_copy(
+            up_out.at[c % 2], gate_ref.at[:, pl.ds(c * span, span)], up_out_sem.at[c]
+        )
+
+    strips = gate_ref.shape[2] // 128
+    unit = 2 * strips * 16
+
+    def untangle(c):
+        if c + 1 < pieces:
+            up_load(c + 1).start()
+        up_load(c).wait()
+        if c >= 2:
+            up_store(c - 2).wait()
+        out_row = lax.broadcasted_iota(jnp.int32, (unit, unit), 0)
+        in_row = lax.broadcasted_iota(jnp.int32, (unit, unit), 1)
+        kind = out_row // (unit // 2)
+        strip = (out_row // 16) & (strips - 1)
+        pick = (out_row & 15) * (2 * strips) + strip * 2 + kind
+        chosen = jnp.where(in_row == pick, 1.0, 0.0).astype(jnp.bfloat16)
+
+        def step(index, carry):
+            sorted_rows = jnp.dot(
+                chosen,
+                up_in[c % 2, pl.ds(index * unit, unit)],
+                preferred_element_type=jnp.float32,
+            ).astype(up_out.dtype)
+            place = pl.ds(index * 16, 16)
+            for kind in (0, 1):
+                for strip in range(strips):
+                    row = (kind * strips + strip) * 16
+                    up_out[c % 2, kind, place, strip * 128 : (strip + 1) * 128] = sorted_rows[
+                        row : row + 16
+                    ]
+            return carry
+
+        lax.fori_loop(0, span // 16, step, 0)
+        up_store(c).start()
+
+    up_load(0).start()
 
     sends = []
 
@@ -211,13 +258,156 @@
             spread_send.at[half, piece, index], spread_recv.at[half, piece, index], own,
         )
 
+    chunks = 2
+
+    def front_part():
+        count, tokens, feature = streams.shape
+        size = tokens // chunks
+        group = 2 * chips
+        width = group * feature
+        head_dim = q_ref.shape[2]
+        rows = q_ref.shape[1]
+        heads = feature // head_dim
+        tree = rows // heads
+        me = lax.axis_index("head")
+        chip = me // 2
+        core = lax.rem(me, 2)
+        turn = 1 - 2 * core
+        sibling = chip * 2 + 1 - core
+
+        def peer(delta):
+            return lax.rem(chip + chips + delta, chips) * 2 + core
+
+        def send_to(source, target, send_sem, recv_sem, head):
+            return pltpu.make_async_remote_copy(
+                src_ref=source,
+                dst_ref=target,
+                send_sem=send_sem,
+                recv_sem=recv_sem,
+                device_id={"head": head},
+                device_id_type=MESH,
+            )
+
+        block = 32
+        for t in range(chunks):
+
+            def mix(index, carry, t=t):
+                here = pl.ds(t * size + index * block, block)
+                mixed = None
+                for s in range(count):
+                    term = hc_in[0, s] * streams[s, here].astype(jnp.float32)
+                    mixed = term if mixed is None else mixed + term
+                mixed_buf[here] = mixed
+                return carry
+
+            lax.fori_loop(0, size // block, mix, 0)
+            mixed = mixed_buf[t * size : (t + 1) * size]
+            stat_all[t, me, 0:1] = transpose_sum(mixed)
+            stat_all[t, me, 1:2] = transpose_sum(mixed * mixed)
+            stat_all[t, me, 2:8] = jnp.zeros((6, size), jnp.float32)
+        enter()
+        waits = {}
+
+        def chunk_rows(t):
+            return pl.ds(t * size, size)
+
+        def lanes(head):
+            return pl.ds(pl.multiple_of(head * feature, feature), feature)
+
+        for t in range(chunks):
+            for step in range(1, group):
+                waits["stat", t, step] = go(
+                    send_to(stat_all.at[t, me], stat_all.at[t, me], front_send.at[t, step],
+                            front_recv.at[t, step], lax.rem(me + step, group)))
+
+        def normalized(t):
+            for step in range(1, group):
+                waits["stat", t, step].wait_recv()
+            total = stat_all[t, 0]
+            for index in range(1, group):
+                total = total + stat_all[t, index]
+            center = total[0:1] / width
+            scale = lax.rsqrt(total[1:2] / width - center * center + 1e-05)
+            row = lax.broadcasted_iota(jnp.int32, total.shape, 0)
+            packed = jnp.where(row == 0, center, jnp.where(row == 1, scale, 0.0))
+            columns[t] = jnp.transpose(packed)
+
+            def step(index, carry):
+                inside = pl.ds(index * block, block)
+                here = pl.ds(t * size + index * block, block)
+                column = columns[t, inside]
+                value = (mixed_buf[here] - column[:, 0:1]) * column[:, 1:2]
+                normed[here] = value.astype(normed.dtype)
+                return carry
+
+            lax.fori_loop(0, size // block, step, 0)
+            mine = normed.at[chunk_rows(t)]
+            view = gathered.at[chunk_rows(t), lanes(me)]
+            waits["fwd", t] = go(send_to(mine, view, pass_send.at[t, 0], pass_recv.at[t, 0], peer(turn)))
+            waits["bwd", t] = go(send_to(mine, view, pass_send.at[t, 1], pass_recv.at[t, 1], peer(-turn)))
+            waits["own", t] = go(send_to(mine, view, copy_send.at[t, 0], copy_recv.at[t, 0], sibling))
+            local = pltpu.make_async_copy(mine, view, own_sem.at[t])
+            local.start()
+            waits["local", t] = local
+
+        def hand_over(t, index, delta):
+            view = gathered.at[chunk_rows(t), lanes(peer(delta))]
+            waits["copy", t, index] = go(
+                send_to(view, view, copy_send.at[t, index], copy_recv.at[t, index], sibling))
+
+        def pass_on(t):
+            waits["fwd", t].wait_recv()
+            view = gathered.at[chunk_rows(t), lanes(peer(-turn))]
+            waits["opp", t] = go(send_to(view, view, pass_send.at[t, 2], pass_recv.at[t, 2], peer(turn)))
+            hand_over(t, 1, -turn)
+            waits["bwd", t].wait_recv()
+            hand_over(t, 2, turn)
+
+        def pass_last(t):
+            waits["opp", t].wait_recv()
+            hand_over(t, 3, 2)
+
+        def project(t):
+            if t == 0:
+                weight_load.wait()
+            waits["own", t].wait_recv()
+            waits["local", t].wait()
+            for index in (1, 2, 3):
+                waits["copy", t, index].wait_recv()
+            here = slice(t * size, (t + 1) * size)
+            for kind, target in enumerate((q_ref, key_ref, value_ref)):
+                product = jnp.dot(gathered[here], weight_buf[kind], preferred_element_type=jnp.float32)
+                for head in range(heads):
+                    value = product[:, head * head_dim : (head + 1) * head_dim]
+                    if kind < 2:
+                        turned = pltpu.roll(value, head_dim // 2, 1)
+                        value = value * cosine[here] + turned * sine[here]
+                    if kind == 0:
+                        value = value * head_dim ** (-0.5)
+                    value = value.astype(target.dtype)
+                    for item in range(size // tree):
+                        target[t * (size // tree) + item, head * tree : (head + 1) * tree] = value[
+                            item * tree : (item + 1) * tree
+                        ]
+            launch(t)
+
+        phases = (normalized, pass_on, pass_last, project)
+        for step in range(len(phases) + chunks - 1):
+            for t in range(chunks):
+                if 0 <= step - t < len(phases):
+                    phases[step - t](t)
+
     halves = (0, 1)
-    for half in halves:
+
+    def launch(half):
         line(half, 0, turn, at(first[half], 0), True)
         line(half, 1, -turn, at(first[half], 0), True)
-    for half in halves:
         cross(half, 0, 0, turn, at(second[half], 0), at(first[half], 0), True)
         cross(half, 0, 1, -turn, at(second[half], 0), at(first[half], 0), True)
+
+    front_part()
+    for load in loads:
+        load.start()
     for half in halves:
         q_all[spot(half, at(second[half], 0), at(first[half], 0))] = q_ref[
             half * block : (half + 1) * block
@@ -225,26 +415,55 @@
     seg_top[...] = jnp.full(seg_top.shape, NEG_FILL, jnp.float32)
     seg_den[...] = jnp.zeros(seg_den.shape, jnp.float32)
     seg_acc[slots] = jnp.zeros(seg_acc.shape[1:], seg_acc.dtype)
+    tree_stat[...] = jnp.zeros(tree_stat.shape, jnp.float32)
+
+    def tree_step(item, carry):
+        found = lax.dot_general(
+            key_ref[item],
+            q_ref[item],
+            (((1,), (1,)), ((), ())),
+            preferred_element_type=jnp.float32,
+        )
+        found = jnp.where(mask_ref[item].astype(jnp.float32) > 0.0, found, NEG_FILL)
+        top = jnp.max(found, axis=0, keepdims=True)
+        weight = jnp.exp(found - top)
+        tree_acc[item] = lax.dot_general(
+            weight.astype(jnp.bfloat16),
+            value_ref[item],
+            (((0,), (0,)), ((), ())),
+            preferred_element_type=jnp.float32,
+        )
+        tree_stat[0, item, :, 0:rows] = top
+        tree_stat[1, item, :, 0:rows] = jnp.sum(weight, axis=0, keepdims=True)
+        return carry
+
+    lax.fori_loop(0, 2 * block, tree_step, 0)
     for half in halves:
         lines[half, 0].wait_recv()
         line(half, 2, turn, at(first[half], -turn))
         cross(half, 1, 0, turn, at(second[half], 0), at(first[half], -turn))
         cross(half, 1, 1, -turn, at(second[half], 0), at(first[half], -turn))
+    untangle(0)
+    untangle(1)
     for half in halves:
         lines[half, 1].wait_recv()
         cross(half, 2, 0, turn, at(second[half], 0), at(first[half], turn))
         cross(half, 2, 1, -turn, at(second[half], 0), at(first[half], turn))
+    untangle(2)
     for half in halves:
         crosses[half, 0, 0].wait_recv()
         cross(half, 0, 2, turn, at(second[half], -turn), at(first[half], 0))
+    untangle(3)
     for half in halves:
         lines[half, 2].wait_recv()
         cross(half, 3, 0, turn, at(second[half], 0), at(first[half], 2))
         cross(half, 3, 1, -turn, at(second[half], 0), at(first[half], 2))
     for piece, delta in ((1, -turn), (2, turn), (3, 2)):
+        untangle(3 + piece)
         for half in halves:
             crosses[half, piece, 0].wait_recv()
             cross(half, piece, 2, turn, at(second[half], -turn), at(first[half], delta))
+    untangle(7)
     for piece in range(4):
         for half in halves:
             crosses[half, piece, 1].wait_recv()
@@ -495,8 +714,6 @@
         p1 = at(first[half], 2)
         tail(half, 0, small.at[half, p1], small_s.at[half, p1], turn)
     lax.fori_loop(1, 2, piece_step, 0)
-    for half in halves:
-        p1 = at(first[half], -turn + 2 + 2)
     lax.fori_loop(2, 4, piece_step, 0)
     for half in halves:
         p1 = at(first[half], -turn)
@@ -522,26 +739,58 @@
         for index in (1, 2):
             for copy in tails[half, index]:
                 copy.wait_recv()
+        tree = [
+            jnp.concatenate(
+                [tree_stat[kind, half * block + item] for item in range(block)], axis=0
+            )
+            for kind in (0, 1)
+        ]
         top, den, weights = weigh(
-            [small_s[half, p1, 0], hop_s[half, 1, 0], hop_s[half, 2, 0]],
-            [small_s[half, p1, 1], hop_s[half, 1, 1], hop_s[half, 2, 1]],
-        )
-        top_ref[half * block : (half + 1) * block] = top
-        den_ref[half * block : (half + 1) * block] = den
+            [small_s[half, p1, 0], hop_s[half, 1, 0], hop_s[half, 2, 0], tree[0]],
+            [small_s[half, p1, 1], hop_s[half, 1, 1], hop_s[half, 2, 1], tree[1]],
+        )
+        lane = lax.broadcasted_iota(jnp.int32, den.shape, 1)
+        inverse = 1.0 / jnp.where(lane < rows, den, 1.0)
 
         def put(item, value, half=half):
-            num_ref[half * block + item] = value
-
-        combine(put, [small.at[half, p1], hop.at[half, 1], hop.at[half, 2]], weights)
+            start = (half * block + item) * half_rows
+            value = value.astype(out_ref.dtype)
+            width = value.shape[1]
+            for head in (0, 1):
+                out_ref[start : start + half_rows, head * width : (head + 1) * width] = value[
+                    head * half_rows : (head + 1) * half_rows
+                ]
+
+        combine(
+            put,
+            [
+                small.at[half, p1],
+                hop.at[half, 1],
+                hop.at[half, 2],
+                tree_acc.at[pl.ds(half * block, block)],
+            ],
+            [weight * inverse for weight in weights],
+        )
     for copy in sends:
         copy.wait_send()
     for half in halves:
         for order in range(4):
             join_copy(half, order).wait_send()
-
-
-def cache_attention(queries, k_pages, v_pages, page_owner, page_fill):
-    req_local, rows, head_dim = queries.shape
+    for c in (pieces - 2, pieces - 1):
+        up_store(c).wait()
+
+
+def cache_attention(
+    streams, hc_in, qkv, up_rows, cosine, sine, tree_mask, k_pages, v_pages, page_owner, page_fill
+):
+    req_local, rows = tree_mask.shape[0:2]
+    head_dim = k_pages.shape[3]
+    tokens, feature = streams.shape[1:3]
+    group = lax.axis_size("head")
+    width = qkv.shape[1]
+    hidden_units = up_rows.shape[0] * 128 // (2 * width)
+    pieces = 8
+    half_tokens = tokens // 2
     slots, keys = k_pages.shape[0], k_pages.shape[1] * k_pages.shape[2]
     devices = lax.axis_size("req")
     side = math.isqrt(devices)
@@ -569,6 +818,25 @@
     unit = (2, side, block, rows, head_dim)
     dma = pltpu.SemaphoreType.DMA
     scratch = [
+        pltpu.VMEM((req_local, rows, head_dim), bf16),
+        pltpu.VMEM((req_local, rows, head_dim), bf16),
+        pltpu.VMEM((req_local, rows, head_dim), bf16),
+        pltpu.VMEM(qkv.shape, bf16),
+        pltpu.VMEM((tokens, feature), f32),
+        pltpu.VMEM((2, group, 8, half_tokens), f32),
+        pltpu.VMEM((2, half_tokens, 8), f32),
+        pltpu.VMEM((tokens, feature), bf16),
+        pltpu.VMEM((tokens, width), bf16),
+        pltpu.VMEM((2, up_rows.shape[0] // pieces, 128), bf16),
+        pltpu.VMEM((2, 2, width // pieces, hidden_units), bf16),
+        dma,
+        dma((2,)),
+        dma((2, group)), dma((2, group)),
+        dma((2, 4)), dma((2, 4)),
+        dma((2, 3)), dma((2, 3)),
+        dma((pieces,)), dma((pieces,)),
+        pltpu.VMEM((req_local, rows, head_dim), f32),
+        pltpu.VMEM((2, req_local, 1, 128), f32),
         pltpu.VMEM((requests, rows, head_dim), bf16),
         pltpu.VMEM((slots, keys, head_dim), bf16),
         pltpu.VMEM((slots, keys, head_dim), bf16),
@@ -604,14 +872,13 @@
     smem = pl.BlockSpec(memory_space=pltpu.SMEM)
     anywhere = pl.BlockSpec(memory_space=pl.ANY)
     return pl.pallas_call(
-        functools.partial(cache_kernel, side),
+        functools.partial(cache_kernel, side, group // 2),
         out_shape=(
-            jax.ShapeDtypeStruct((req_local, rows, head_dim), f32),
-            jax.ShapeDtypeStruct((req_local, 128), f32),
-            jax.ShapeDtypeStruct((req_local, 128), f32),
+            jax.ShapeDtypeStruct((req_local * rows // 2, 2 * head_dim), bf16),
+            jax.ShapeDtypeStruct((2, width, hidden_units), bf16),
         ),
-        in_specs=[smem, smem, vmem, anywhere, anywhere],
-        out_specs=(vmem, vmem, vmem),
+        in_specs=[smem] * 3 + [vmem] * 4 + [anywhere] * 4,
+        out_specs=(vmem, anywhere),
         scratch_shapes=scratch,
         compiler_params=pltpu.CompilerParams(
             collective_id=0, has_side_effects=True, vmem_limit_bytes=56 << 20
@@ -619,7 +886,13 @@
     )(
         table,
         last,
-        queries,
+        hc_in,
+        streams,
+        cosine,
+        sine,
+        tree_mask,
+        qkv,
+        up_rows,
         k_pages.reshape(slots, keys, head_dim),
         v_pages.reshape(slots, keys, head_dim),
     )
@@ -808,9 +1081,9 @@
     def remixed(layer, values, delta):
         result = []
         for target in range(count):
-            total = hc_out[layer * count + target] * delta
+            total = hc_out[layer, target] * delta
             for source in range(count):
-                weight = hc_mix[(layer * count + source) * count + target]
+                weight = hc_mix[layer, source, target]
                 if source == target:
                     weight = weight + 1.0
                 total = total + weight * values[source]
@@ -836,7 +1109,7 @@
             mixed = None
             for s in range(count):
                 first_buf[s, rows] = result[s]
-                term = hc_in[count + s] * result[s]
+                term = hc_in[1, s] * result[s]
                 mixed = term if mixed is None else mixed + term
             mixed_buf[rows] = mixed
             return carry
@@ -1018,9 +1291,9 @@
             collective_id=1, has_side_effects=True, vmem_limit_bytes=60 << 20
         ),
     )(
-        hc_in.reshape(-1),
-        hc_mix.reshape(-1),
-        hc_out.reshape(-1),
+        hc_in,
+        hc_mix,
+        hc_out,
         accepted,
         attended,
         streams,
@@ -1253,74 +1526,41 @@
     accepted_index,
 ):
     tokens_local = streams.shape[0]
-    feature_local = streams.shape[2]
-    width = qkv_weight.shape[0]
     req_local = cache_len.shape[0]
     tree_size = tree_parent.shape[1]
-    slot_count = k_pages.shape[0]
-    page_size = k_pages.shape[1]
     heads_local = k_pages.shape[2]
     head_dim = k_pages.shape[3]
     draft_count = draft_weight.shape[0]
     all_requests = req_local * lax.axis_size("req")
     reach = ancestors(tree_parent)
-    depth = (jnp.sum(reach, axis=2) - 1.0).astype(jnp.int32)
+    depth = (jnp.sum(reach.astype(jnp.float32), axis=1) - 1.0).astype(jnp.int32)
     positions = (cache_len[:, None] + depth).reshape(tokens_local)
-    stream_vals = streams.astype(jnp.float32)
-    mixed_in = blend(stream_vals, hc_in[0])
-    stat_sum, stat_square = lax.psum(
-        (jnp.sum(mixed_in, axis=1), jnp.sum(mixed_in * mixed_in, axis=1)), "head"
+    cosine, sine = turns(positions, head_dim)
+    same_head = jnp.eye(heads_local, dtype=jnp.bfloat16)
+    tree_mask = (same_head[None, :, None, :, None] * reach[:, None, :, None, :]).reshape(
+        req_local, heads_local * tree_size, heads_local * tree_size
     )
-    normed = normalize(mixed_in, stat_sum[:, None], stat_square[:, None], width).astype(
-        jnp.bfloat16
+    by_stream = jnp.transpose(streams, (1, 0, 2))
+    width, kinds, inner = up_gate.shape
+    up_rows = jnp.transpose(up_gate.reshape(width, kinds, inner // 128, 128), (0, 2, 1, 3)).reshape(
+        -1, 128
     )
-    qkv_flat = qkv_weight.reshape(width, -1)
-    normed_full = lax.all_gather(normed, "head", axis=1, tiled=True)
-    gate_up = jnp.transpose(up_gate, (1, 0, 2))
-    normed_full, gate_up = lax.optimization_barrier((normed_full, gate_up))
-    projected = fold_rows(qkv_flat, normed_full)
-    projected = projected.reshape(tokens_local, 3, heads_local, head_dim)
-    queries = (rotate(projected[:, 0], positions) * head_dim ** (-0.5)).astype(jnp.bfloat16)
-    keys_new = rotate(projected[:, 1], positions).astype(jnp.bfloat16)
-    values_new = projected[:, 2].astype(jnp.bfloat16)
-    query_rows = (
-        queries.reshape(req_local, tree_size, heads_local, head_dim)
-        .transpose(0, 2, 1, 3)
-        .reshape(req_local, heads_local * tree_size, head_dim)
-    )
-    own_sum, own_top, own_den = cache_attention(
-        query_rows, k_pages, v_pages, page_owner, page_fill
-    )
-    own_sum = own_sum.reshape(req_local, heads_local, tree_size, head_dim).transpose(0, 2, 1, 3)
-    used = heads_local * tree_size
-    own_top = own_top[:, :used].reshape(req_local, heads_local, tree_size).transpose(0, 2, 1)
-    own_den = own_den[:, :used].reshape(req_local, heads_local, tree_size).transpose(0, 2, 1)
-    query_own = queries.reshape(req_local, tree_size, heads_local, head_dim)
-    keys_own = keys_new.reshape(req_local, tree_size, heads_local, head_dim)
-    values_own = values_new.reshape(req_local, tree_size, heads_local, head_dim)
-    tree_scores = jnp.einsum(
-        "jqhd,jkhd->jqhk", query_own, keys_own, preferred_element_type=jnp.float32
-    )
-    tree_mask = (reach > 0)[:, :, None, :]
-    tree_scores = jnp.where(tree_mask, tree_scores, NEG_FILL)
-    top = jnp.maximum(own_top, jnp.max(tree_scores, axis=3))
-    carried = jnp.exp(own_top - top)
-    tree_weights = jnp.where(tree_mask, jnp.exp(tree_scores - top[..., None]), 0.0)
-    denominator = own_den * carried + jnp.sum(tree_weights, axis=3)
-    numerator = own_sum * carried[..., None] + jnp.einsum(
-        "jqhk,jkhd->jqhd",
-        tree_weights.astype(jnp.bfloat16),
-        values_own,
-        preferred_element_type=jnp.float32,
-    )
-    attended = (
-        (numerator / denominator[..., None])
-        .astype(jnp.bfloat16)
-        .reshape(tokens_local, heads_local * head_dim)
+    attended, gate_up = cache_attention(
+        by_stream,
+        hc_in,
+        jnp.transpose(qkv_weight, (1, 0, 2)),
+        up_rows,
+        cosine,
+        sine,
+        tree_mask,
+        k_pages,
+        v_pages,
+        page_owner,
+        page_fill,
     )
     fresh, final_local = layer(
         attended,
-        jnp.transpose(streams, (1, 0, 2)),
+        by_stream,
         hc_in,
         hc_mix,
         hc_out,

time: 302 us -> 252 us (0.83); the launches traced: 298 us -> 251 us
  Pallas kernels: 184 us -> 214 us
  local copies, waits for them, and re-layouts: 37.6 us -> 11.7 us
  blocking collectives: 14.7 us -> 0 us
  between operations: 14.6 us -> 0.79 us
  waiting for transfers between devices: 18.9 us -> 9.91 us
  other arithmetic: 13.6 us -> 6.51 us
  matrix products: 8.78 us -> 2.42 us
    pallas_call x1, Pallas kernels: 86.9 us -> 117 us  [cache_attention(): pl.pallas_call(functools.partial(cache_kernel, side, group // 2), out_sha...]
    psum x1 -> x0, blocking collectives: 14.7 us -> none  [on_device(): lax.psum((jnp.sum(mixed_in, axis=1), jnp.sum(mixed_in * mixed_in, axis=1)...]
    unnamed x30 -> x10, local copies, waits for them, and re-layouts: 20.7 us -> 7.31 us
    all_gather x1 -> x0, waiting for transfers between devices: 8.97 us -> none  [on_device(): normed_full = lax.all_gather(normed, 'head', axis=1, tiled=True)]
    dot_general x9 -> x3, matrix products: 8.78 us -> 2.42 us  [ancestors(): jnp.einsum('jki,jil->jkl', reach, reach, preferred_element_type=jnp.float32)]
    concatenate x8 -> x0, local copies, waits for them, and re-layouts: 6.09 us -> none  [rotate(): jnp.concatenate([first * cosine - second * sine, second * cosine + first...]
    reshape x5 -> x0, local copies, waits for them, and re-layouts: 4.26 us -> none  [the longest x1 1.3 us: layer(): hc_out.reshape(-1)]
    reduce_sum x3 -> x0, other arithmetic: 3.15 us -> none  [the longest x1 2.72 us: on_device(): jnp.sum(mixed_in, axis=1)]
  transfers between devices with their start and end apart: 2 -> 1, of which waited for: 2 -> 1; matrix products, arithmetic and copies ran while one was open for 9% -> 1% of each run, Pallas kernels for 0% -> 0%
where the time goes in v3:
time: 252 us; the launch traced here: 251 us
  Pallas kernels  214 us (85%)
  local copies, waits for them, and re-layouts  11.7 us (5%)
  waiting for transfers between devices  9.91 us (4%)
  other arithmetic  6.51 us (3%)
  starting transfers between devices  5.73 us (2%)
    pallas_call x1, Pallas kernels, cache_attention(): pl.pallas_call(functools.partial(cache_kernel, side, group // 2), out_sha...  117 us
    pallas_call x1, Pallas kernels, layer(): pl.pallas_call(functools.partial(layer_kernel, chips, chunks), out_shape=...  66 us
    pallas_call x1, Pallas kernels, draft_logits(): pl.pallas_call(functools.partial(draft_kernel, group // 2), out_shape=jax...  31.1 us
    all_to_all x1, waiting for transfers between devices, on_device(): lax.all_to_all(logits_local, ('req', 'head'), split_axis=0, concat_axis=2...  9.91 us
    unnamed x10, local copies, waits for them, and re-layouts  7.31 us
    all_to_all x1, starting transfers between devices, on_device(): lax.all_to_all(logits_local, ('req', 'head'), split_axis=0, concat_axis=2...  5.73 us
  transfers between devices with their start and end apart: 1, of which 1 were waited for; matrix products, arithmetic and copies ran while one was open for 1% of the time, Pallas kernels for 0%

profile of v3, /device:TPU:1, one launch (start us, length us, event | category | flops | bytes accessed | tf_op | source)
XLA Modules:
  0.0 251.3 jit_solution(1358035305170858282)
XLA Ops:
  0.6 0.0 copy-start.3
  0.7 0.8 compare_select_fusion.5
  1.5 0.2 convert_reduce_fusion.3
  1.7 0.7 select_reduce_fusion.table
  2.3 0.1 mul.93
  2.4 0.1 mul.94
  2.5 1.4 fusion.1
  4.0 0.5 fusion.3
  4.5 0.5 convert_reduce_fusion
  5.0 0.7 add_convert_fusion
  5.7 0.1 convert_element_type.81
  5.8 0.5 mul.96
  6.3 0.3 mul.97
  6.6 1.3 copy.33
  8.0 0.1 convert_reduce_fusion.1
  8.1 0.6 compare_select_fusion.6.last
  8.7 0.8 broadcast_multiply_fusion.mask_ref
  9.5 1.4 fusion.16
  10.9 1.2 pad_maximum_fusion
  12.1 117.2 %shard_map.176 = (bf16[768,256]{1,0:T(8,128)(2,1)}, bf16[2,2048,1024]{2,1,0:T(8,128)(2,1)}) custom-call(s32[48]{0:T(128)} %select_reduce_fusion.table, s32[256]{0:T(256)} %compare_select_fusion.6.last, f32[2,4]{1,0:T(2,128)} %hc_in.3, bf16[4,768,256]{2,1,0:T(8,128)(2,1)} %bitcast.25, f32[768,128]{1,0:T(8,128)} %get-tuple-element.25.cosine, ...), custom_call_target="tpu_custom_call" | custom-call | tf_op jit(solution)/shard_map/pallas_call | solution.py:874
  129.3 0.0 copy-start
  129.3 66.0 %shard_map.177 = (bf16[4,768,256]{2,1,0:T(8,128)(2,1)}, f32[32,256]{1,0:T(8,128)}) custom-call(f32[2,4]{1,0:T(2,128)} %hc_in.3, f32[2,4,4]{2,1,0:T(4,128)} %hc_mix.1, f32[2,4]{1,0:T(2,128)} %hc_out.1, s32[16]{0:T(128)} %accepted.1, bf16[768,256]{1,0:T(8,128)(2,1)} %get-tuple-element.6.attended, bf16[4,768,256]{2,1,0:T(8,128)(2,1)} %bitcast.26, ...), custom_call_target="tpu_custom_call" | custom-call | tf_op jit(solution)/shard_map/pallas_call | solution.py:1281
  195.3 0.0 copy-start.1
  195.3 1.4 copy-done.1
  196.7 0.8 copy-done.2
  197.5 31.1 %shard_map.178 = bf16[512,393]{1,0:T(8,128)(2,1)S(1)} custom-call(f32[32,256]{1,0:T(8,128)S(1)} %copy-done.2, bf16[2,2048,256]{2,1,0:T(8,128)(2,1)S(1)} %copy-done, bf16[393,2048]{1,0:T(8,128)(2,1)S(1)} %bitcast.24), custom_call_target="tpu_custom_call" | custom-call | tf_op jit(solution)/shard_map/pallas_call | solution.py:1486
  228.6 1.0 reshape.150
  229.6 5.7 %all-to-all-start = ((bf16[256,2,393]{2,1,0:T(2,128)(2,1)}), bf16[256,2,393]{2,1,0:T(2,128)(2,1)S(1)}, u32[]{:S(2)}, u32[]{:S(2)}) async-start(bf16[256,2,393]{2,1,0:T(2,128)(2,1)} %reshape.150), calls=%async_computation | async-start | bytes 1048576 | tf_op jit(solution)/shard_map/all_to_all | solution.py:1576
  235.3 3.8 %copy.30 = bf16[768,4,256]{2,1,0:T(4,128)(2,1)} copy(bf16[768,4,256]{2,0,1:T(8,128)(2,1)} %bitcast.33) | data formatting | bytes 3145728
  239.1 9.9 %all-to-all-done = bf16[256,2,393]{2,1,0:T(2,128)(2,1)S(1)} async-done(((bf16[256,2,393]{2,1,0:T(2,128)(2,1)}), bf16[256,2,393]{2,1,0:T(2,128)(2,1)S(1)}, u32[]{:S(2)}, u32[]{:S(2)}) %all-to-all-start) | async-done | bytes 402464 | tf_op jit(solution)/shard_map/all_to_all | solution.py:1576
  249.0 0.1 copy.34
  249.1 2.1 reshape.151
  (7 shorter events, 0.0 us)
Async XLA Ops:
  0.6 6.0 %copy-start.3 = (bf16[768,4,256]{2,1,0:T(4,128)(2,1)S(1)}, bf16[768,4,256]{2,1,0:T(4,128)(2,1)}, u32[]{:S(2)}) copy-start(bf16[768,4,256]{2,1,0:T(4,128)(2,1)} %param.17) | copy-start | bytes 4718596
  129.3 66.0 %copy-start = (bf16[2,2048,256]{2,1,0:T(8,128)(2,1)S(1)}, bf16[2,2048,256]{2,1,0:T(8,128)(2,1)}, u32[]{:S(2)}) copy-start(bf16[2,2048,256]{2,1,0:T(8,128)(2,1)} %weight_hbm.1) | copy-start | bytes 6291460
  195.3 1.4 copy-start.1
  196.7 0.8 copy-start.2
  229.6 19.4 %all-to-all-start = ((bf16[256,2,393]{2,1,0:T(2,128)(2,1)}), bf16[256,2,393]{2,1,0:T(2,128)(2,1)S(1)}, u32[]{:S(2)}, u32[]{:S(2)}) async-start(bf16[256,2,393]{2,1,0:T(2,128)(2,1)} %reshape.150), calls=%async_computation | async-start | bytes 1048576 | tf_op jit(solution)/shard_map/all_to_all | solution.py:1576

commit v4 on v3

--- a/solution.py
+++ b/solution.py
@@ -575,7 +575,9 @@
             stats[group, 1, piece * block : (piece + 1) * block] = jnp.concatenate(dens, axis=0)
         return carry
 
-    lax.fori_loop(0, 2 * side, place_step, 0)
+    for half in halves:
+        for delta in (2, -turn):
+            place_step(half * side + at(second[half], delta), 0)
 
     def part(half, p2, p1):
         return parts.at[spot(half, p2, p1)]
@@ -612,6 +614,10 @@
             near[half, order] = go(
                 remote(part(half, at(second[half], -turn), p1), single.at[half, p1],
                        near_send.at[half, order], near_recv.at[half, order], down))
+
+    for half in halves:
+        for delta in (turn, 0):
+            place_step(half * side + at(second[half], delta), 0)
 
     for half in halves:
         stat_copies[half, 0].wait_recv()
@@ -915,8 +921,25 @@
     out_hbm,
     gate_hbm,
     down_hbm,
+    weight_hbm,
+    vocab_hbm,
     fresh_ref,
+    logits_ref,
     final_ref,
+    final_all,
+    weight_buf,
+    vocab_buf,
+    shards,
+    logits_acc,
+    draft_sem,
+    sum_send,
+    sum_recv,
+    draft_send,
+    draft_recv,
+    hand_send,
+    hand_recv,
+    loop_send,
+    loop_recv,
     out_buf,
     gate_buf,
     down_buf,
@@ -998,14 +1021,29 @@
                 down_hbm.at[:, pl.ds(index * feature, feature)], down_buf.at[index], load_sem.at[2, index]
             )
         )
-    for load in loads:
+    draft_loads = [pltpu.make_async_copy(weight_hbm, weight_buf, draft_sem.at[0])]
+    for index in range(group):
+        draft_loads.append(
+            pltpu.make_async_copy(
+                vocab_hbm.at[:, pl.ds(index * feature, feature)],
+                vocab_buf.at[index],
+                draft_sem.at[1 + index],
+            )
+        )
+    for load in loads + draft_loads:
         load.start()
     barrier = pltpu.get_barrier_semaphore()
+    home_index = lax.axis_index("req")
+    peers = shards.shape[1] // final_ref.shape[0]
     for step in range(1, group):
         pl.semaphore_signal(
             barrier, inc=1, device_id={"head": lax.rem(me + step, group)}, device_id_type=MESH
         )
-    pl.semaphore_wait(barrier, group - 1)
+    for step in range(1, peers):
+        pl.semaphore_signal(
+            barrier, inc=1, device_id={"req": lax.rem(home_index + step, peers)}, device_id_type=MESH
+        )
+    pl.semaphore_wait(barrier, group + peers - 2)
 
     sends = []
 
@@ -1232,13 +1270,148 @@
         for copy_index in range(repeats):
             place = item * repeats + copy_index
             final_ref[place : place + 1] = row
+
+    def draft_part():
+        rows, feature = final_ref.shape
+        group = 2 * chips
+        width = group * feature
+        devices = shards.shape[1] // rows
+        me = lax.axis_index("head")
+        home = lax.axis_index("req")
+        chip = me // 2
+        core = lax.rem(me, 2)
+        turn = 1 - 2 * core
+        sibling = chip * 2 + 1 - core
+
+        def peer(delta):
+            return lax.rem(chip + chips + delta, chips) * 2 + core
+
+        def send_to(source, target, send_sem, recv_sem, device):
+            return pltpu.make_async_remote_copy(
+                src_ref=source,
+                dst_ref=target,
+                send_sem=send_sem,
+                recv_sem=recv_sem,
+                device_id=device,
+                device_id_type=MESH,
+            )
+
+        sums = []
+        for step in range(1, group):
+            sums.append(
+                go(send_to(final_ref, final_all.at[me], sum_send.at[step], sum_recv.at[step],
+                           {"head": lax.rem(me + step, group)}))
+            )
+        final_all[me] = final_ref[...]
+        draft_loads[0].wait()
+        for copy in sums:
+            copy.wait_recv()
+        center = jnp.zeros((rows, 1), jnp.float32)
+        square = jnp.zeros((rows, 1), jnp.float32)
+        for index in range(group):
+            values = final_all[index]
+            center = center + jnp.sum(values, axis=1, keepdims=True)
+            square = square + jnp.sum(values * values, axis=1, keepdims=True)
+        center = center / width
+        scale = lax.rsqrt(square / width - center * center + 1e-05)
+        branches = []
+        for kind in range(2):
+            branch = jnp.zeros((rows, feature), jnp.float32)
+            for index in range(group):
+                values = ((final_all[index] - center) * scale).astype(jnp.bfloat16)
+                branch = branch + jnp.dot(
+                    values,
+                    weight_buf[kind, index * feature : (index + 1) * feature],
+                    preferred_element_type=jnp.float32,
+                )
+            branches.append(branch)
+        odd = (lax.broadcasted_iota(jnp.int32, (rows, feature), 0) & 1) == 1
+        branch = jnp.where(odd, branches[1], branches[0])
+        drafted = (final_ref[...] - center) * scale + branch * lax.logistic(branch)
+        mine = shards.at[me, pl.ds(pl.multiple_of(home * rows, rows), rows)]
+        mine[...] = drafted.astype(shards.dtype)
+        drafts = []
+        for step in range(1, devices):
+            drafts.append(
+                go(send_to(mine, mine, draft_send.at[step], draft_recv.at[step],
+                           {"req": lax.rem(home + step, devices)}))
+            )
+        for copy in drafts:
+            copy.wait_recv()
+
+        def shard(head):
+            return shards.at[head]
+
+        def ring(index, delta, source):
+            return go(send_to(shard(source), shard(source), loop_send.at[index], loop_recv.at[index],
+                              {"head": peer(delta)}))
+
+        def hand_over(index, source):
+            return go(send_to(shard(source), shard(source), hand_send.at[index], hand_recv.at[index],
+                              {"head": sibling}))
+
+        fwd = ring(0, turn, me)
+        bwd = ring(1, -turn, me)
+        hands = [hand_over(0, me)]
+        for load in draft_loads[1:]:
+            load.wait()
+
+        def add(head, first=False):
+            value = lax.dot_general(
+                shards[head],
+                vocab_buf[head],
+                (((1,), (1,)), ((), ())),
+                preferred_element_type=jnp.float32,
+            )
+            logits_acc[...] = value if first else logits_acc[...] + value
+
+        add(me, True)
+        fwd.wait_recv()
+        opp = ring(2, turn, peer(-turn))
+        hands.append(hand_over(1, peer(-turn)))
+        bwd.wait_recv()
+        hands.append(hand_over(2, peer(turn)))
+        add(peer(-turn))
+        hands[0].wait_recv()
+        add(sibling)
+        add(peer(turn))
+        opp.wait_recv()
+        hands.append(hand_over(3, peer(2)))
+        hands[1].wait_recv()
+
+        def across(delta):
+            return lax.rem(chip + chips + delta, chips) * 2 + 1 - core
+
+        add(across(turn))
+        hands[2].wait_recv()
+        add(across(-turn))
+        add(peer(2))
+        hands[3].wait_recv()
+        add(across(2))
+        logits_ref[...] = logits_acc[...].astype(logits_ref.dtype)
+
+    draft_part()
     for copy in sends:
         copy.wait_send()
 
 
 def layer(
-    attended, streams, hc_in, hc_mix, hc_out, out_weight, gate_up, down_weight, accepted, repeats
+    attended,
+    streams,
+    hc_in,
+    hc_mix,
+    hc_out,
+    out_weight,
+    gate_up,
+    down_weight,
+    accepted,
+    draft_weight,
+    lm_head,
 ):
+    repeats = draft_weight.shape[0]
+    rows = accepted.shape[0] * repeats
+    devices = lax.axis_size("req")
+    vocab = lm_head.shape[1]
     tokens, feature = attended.shape
     count = streams.shape[0]
     group = lax.axis_size("head")
@@ -1254,6 +1427,17 @@
     smem = pl.BlockSpec(memory_space=pltpu.SMEM)
     anywhere = pl.BlockSpec(memory_space=pl.ANY)
     scratch = [
+        pltpu.VMEM((rows, feature), f32),
+        pltpu.VMEM((group, rows, feature), f32),
+        pltpu.VMEM(draft_weight.shape, bf16),
+        pltpu.VMEM((group, vocab, feature), bf16),
+        pltpu.VMEM((group, devices * rows, feature), bf16),
+        pltpu.VMEM((devices * rows, vocab), f32),
+        dma((1 + group,)),
+        dma((group,)), dma((group,)),
+        dma((devices,)), dma((devices,)),
+        dma((4,)), dma((4,)),
+        dma((3,)), dma((3,)),
         pltpu.VMEM((group, feature, feature), bf16),
         pltpu.VMEM((2 * strips, width, feature), bf16),
         pltpu.VMEM((group, inner, feature), bf16),
@@ -1282,9 +1466,9 @@
         functools.partial(layer_kernel, chips, chunks),
         out_shape=(
             jax.ShapeDtypeStruct((count, tokens, feature), bf16),
-            jax.ShapeDtypeStruct((accepted.shape[0] * repeats, feature), f32),
+            jax.ShapeDtypeStruct((devices * rows, vocab), bf16),
         ),
-        in_specs=[smem] * 4 + [vmem, vmem, anywhere, anywhere, anywhere],
+        in_specs=[smem] * 4 + [vmem, vmem] + [anywhere] * 5,
         out_specs=(vmem, vmem),
         scratch_shapes=scratch,
         compiler_params=pltpu.CompilerParams(
@@ -1300,210 +1484,9 @@
         out_weight,
         gate_up,
         down_weight,
+        draft_weight,
+        jnp.transpose(lm_head),
     )
-
-
-def draft_kernel(
-    chips,
-    final_ref,
-    weight_hbm,
-    vocab_hbm,
-    logits_ref,
-    final_all,
-    weight_buf,
-    vocab_buf,
-    gathered,
-    total,
-    load_sem,
-    sum_send,
-    sum_recv,
-    draft_send,
-    draft_recv,
-    copy_send,
-    copy_recv,
-    pass_send,
-    pass_recv,
-):
-    rows, feature = final_ref.shape
-    group = 2 * chips
-    width = group * feature
-    devices = gathered.shape[1] // rows
-    me = lax.axis_index("head")
-    home = lax.axis_index("req")
-    chip = me // 2
-    core = lax.rem(me, 2)
-    turn = 1 - 2 * core
-    sibling = chip * 2 + 1 - core
-
-    def peer(delta):
-        return lax.rem(chip + chips + delta, chips) * 2 + core
-
-    def send_to(source, target, send_sem, recv_sem, device):
-        return pltpu.make_async_remote_copy(
-            src_ref=source,
-            dst_ref=target,
-            send_sem=send_sem,
-            recv_sem=recv_sem,
-            device_id=device,
-            device_id_type=MESH,
-        )
-
-    loads = [pltpu.make_async_copy(weight_hbm, weight_buf, load_sem.at[0])]
-    for index in range(group):
-        loads.append(
-            pltpu.make_async_copy(
-                vocab_hbm.at[:, pl.ds(index * feature, feature)],
-                vocab_buf.at[index],
-                load_sem.at[1 + index],
-            )
-        )
-    for load in loads:
-        load.start()
-    barrier = pltpu.get_barrier_semaphore()
-    for step in range(1, group):
-        pl.semaphore_signal(
-            barrier, inc=1, device_id={"head": lax.rem(me + step, group)}, device_id_type=MESH
-        )
-    for step in range(1, devices):
-        pl.semaphore_signal(
-            barrier, inc=1, device_id={"req": lax.rem(home + step, devices)}, device_id_type=MESH
-        )
-    pl.semaphore_wait(barrier, group + devices - 2)
-
-    sends = []
-
-    def go(copy):
-        copy.start()
-        sends.append(copy)
-        return copy
-
-    sums = []
-    for step in range(1, group):
-        sums.append(
-            go(send_to(final_ref, final_all.at[me], sum_send.at[step], sum_recv.at[step],
-                       {"head": lax.rem(me + step, group)}))
-        )
-    final_all[me] = final_ref[...]
-    loads[0].wait()
-    for copy in sums:
-        copy.wait_recv()
-    center = jnp.zeros((rows, 1), jnp.float32)
-    square = jnp.zeros((rows, 1), jnp.float32)
-    for index in range(group):
-        values = final_all[index]
-        center = center + jnp.sum(values, axis=1, keepdims=True)
-        square = square + jnp.sum(values * values, axis=1, keepdims=True)
-    center = center / width
-    scale = lax.rsqrt(square / width - center * center + 1e-05)
-    branches = []
-    for kind in range(2):
-        branch = jnp.zeros((rows, feature), jnp.float32)
-        for index in range(group):
-            values = ((final_all[index] - center) * scale).astype(jnp.bfloat16)
-            branch = branch + jnp.dot(
-                values,
-                weight_buf[kind, index * feature : (index + 1) * feature],
-                preferred_element_type=jnp.float32,
-            )
-        branches.append(branch)
-    odd = (lax.broadcasted_iota(jnp.int32, (rows, feature), 0) & 1) == 1
-    branch = jnp.where(odd, branches[1], branches[0])
-    drafted = (final_ref[...] - center) * scale + branch * lax.logistic(branch)
-    mine = gathered.at[me, pl.ds(pl.multiple_of(home * rows, rows), rows)]
-    mine[...] = drafted.astype(gathered.dtype)
-    drafts = []
-    for step in range(1, devices):
-        drafts.append(
-            go(send_to(mine, mine, draft_send.at[step], draft_recv.at[step],
-                       {"req": lax.rem(home + step, devices)}))
-        )
-    for copy in drafts:
-        copy.wait_recv()
-
-    def shard(head):
-        return gathered.at[head]
-
-    def ring(index, delta, source):
-        return go(send_to(shard(source), shard(source), pass_send.at[index], pass_recv.at[index],
-                          {"head": peer(delta)}))
-
-    def hand_over(index, source):
-        return go(send_to(shard(source), shard(source), copy_send.at[index], copy_recv.at[index],
-                          {"head": sibling}))
-
-    fwd = ring(0, turn, me)
-    bwd = ring(1, -turn, me)
-    hands = [hand_over(0, me)]
-    for load in loads[1:]:
-        load.wait()
-
-    def add(head, first=False):
-        value = lax.dot_general(
-            gathered[head],
-            vocab_buf[head],
-            (((1,), (1,)), ((), ())),
-            preferred_element_type=jnp.float32,
-        )
-        total[...] = value if first else total[...] + value
-
-    add(me, True)
-    fwd.wait_recv()
-    opp = ring(2, turn, peer(-turn))
-    hands.append(hand_over(1, peer(-turn)))
-    bwd.wait_recv()
-    hands.append(hand_over(2, peer(turn)))
-    add(peer(-turn))
-    hands[0].wait_recv()
-    add(sibling)
-    add(peer(turn))
-    opp.wait_recv()
-    hands.append(hand_over(3, peer(2)))
-    hands[1].wait_recv()
-
-    def across(delta):
-        return lax.rem(chip + chips + delta, chips) * 2 + 1 - core
-
-    add(across(turn))
-    hands[2].wait_recv()
-    add(across(-turn))
-    add(peer(2))
-    hands[3].wait_recv()
-    add(across(2))
-    logits_ref[...] = total[...].astype(logits_ref.dtype)
-    for copy in sends:
-        copy.wait_send()
-
-
-def draft_logits(final_rows, draft_weight, lm_head):
-    rows, feature = final_rows.shape
-    group = lax.axis_size("head")
-    devices = lax.axis_size("req")
-    width, vocab = lm_head.shape
-    bf16, f32 = jnp.bfloat16, jnp.float32
-    dma = pltpu.SemaphoreType.DMA
-    vmem = pl.BlockSpec(memory_space=pltpu.VMEM)
-    anywhere = pl.BlockSpec(memory_space=pl.ANY)
-    return pl.pallas_call(
-        functools.partial(draft_kernel, group // 2),
-        out_shape=jax.ShapeDtypeStruct((devices * rows, vocab), bf16),
-        in_specs=[vmem, anywhere, anywhere],
-        out_specs=vmem,
-        scratch_shapes=[
-            pltpu.VMEM((group, rows, feature), f32),
-            pltpu.VMEM(draft_weight.shape, bf16),
-            pltpu.VMEM((group, vocab, feature), bf16),
-            pltpu.VMEM((group, devices * rows, feature), bf16),
-            pltpu.VMEM((devices * rows, vocab), f32),
-            dma((1 + group,)),
-            dma((group,)), dma((group,)),
-            dma((devices,)), dma((devices,)),
-            dma((4,)), dma((4,)),
-            dma((3,)), dma((3,)),
-        ],
-        compiler_params=pltpu.CompilerParams(
-            collective_id=2, has_side_effects=True, vmem_limit_bytes=40 << 20
-        ),
-    )(final_rows, draft_weight, jnp.transpose(lm_head))
 
 
 def on_device(
@@ -1558,7 +1541,7 @@
         page_owner,
         page_fill,
     )
-    fresh, final_local = layer(
+    fresh, logits_local = layer(
         attended,
         by_stream,
         hc_in,
@@ -1568,10 +1551,10 @@
         gate_up,
         down_weight,
         accepted_index,
-        draft_count,
+        draft_weight,
+        lm_head,
     )
     new_streams = jnp.transpose(fresh, (1, 0, 2))
-    logits_local = draft_logits(final_local, draft_weight, lm_head)
     logits_local = logits_local.reshape(all_requests, draft_count, -1)
     logits = lax.all_to_all(
         logits_local, ("req", "head"), split_axis=0, concat_axis=2, tiled=True

time: 252 us -> 249 us (0.988)
    pallas_call x1 -> x0, Pallas kernels: 31.1 us -> none  [draft_logits(): pl.pallas_call(functools.partial(draft_kernel, group // 2), out_shape=jax...]
    pallas_call x1, Pallas kernels: 66 us -> 94.5 us  [layer(): pl.pallas_call(functools.partial(layer_kernel, chips, chunks), out_shape=...]
    unnamed x10 -> x6, local copies, waits for them, and re-layouts: 7.31 us -> 3.72 us
where the time goes in v4:
time: 249 us; the launch traced here: 248 us
  Pallas kernels  212 us (85%)
  waiting for transfers between devices  11.3 us (5%)
  local copies, waits for them, and re-layouts  9.28 us (4%)
  other arithmetic  6.51 us (3%)
  starting transfers between devices  6.02 us (2%)
    pallas_call x1, Pallas kernels, cache_attention(): pl.pallas_call(functools.partial(cache_kernel, side, group // 2), out_sha...  117 us
    pallas_call x1, Pallas kernels, layer(): pl.pallas_call(functools.partial(layer_kernel, chips, chunks), out_shape=...  94.5 us
    all_to_all x1, waiting for transfers between devices, on_device(): lax.all_to_all(logits_local, ('req', 'head'), split_axis=0, concat_axis=2...  11.3 us
    all_to_all x1, starting transfers between devices, on_device(): lax.all_to_all(logits_local, ('req', 'head'), split_axis=0, concat_axis=2...  6.02 us
  transfers between devices with their start and end apart: 1, of which 1 were waited for; matrix products, arithmetic and copies ran while one was open for 1% of the time, Pallas kernels for 0%

profile of v4, /device:TPU:1, one launch (start us, length us, event | category | flops | bytes accessed | tf_op | source)
XLA Modules:
  0.0 248.2 jit_solution(6616931386418946557)
XLA Ops:
  0.6 0.0 copy-start
  0.7 0.8 compare_select_fusion.5
  1.5 0.2 convert_reduce_fusion.3
  1.7 0.7 select_reduce_fusion.table
  2.3 0.1 mul.93
  2.4 0.1 mul.94
  2.5 1.4 fusion.1
  4.0 0.5 fusion.3
  4.5 0.5 convert_reduce_fusion
  5.0 0.7 add_convert_fusion
  5.7 0.1 convert_element_type.81
  5.8 0.5 mul.96
  6.3 0.3 mul.97
  6.6 0.0 copy-done
  6.6 1.3 copy.33
  8.0 0.1 convert_reduce_fusion.1
  8.1 0.6 compare_select_fusion.6.last
  8.7 0.8 broadcast_multiply_fusion.mask_ref
  9.5 1.4 fusion.16
  10.9 1.2 pad_maximum_fusion
  12.1 117.4 %shard_map.176 = (bf16[768,256]{1,0:T(8,128)(2,1)}, bf16[2,2048,1024]{2,1,0:T(8,128)(2,1)}) custom-call(s32[48]{0:T(128)} %select_reduce_fusion.table, s32[256]{0:T(256)} %compare_select_fusion.6.last, f32[2,4]{1,0:T(2,128)} %hc_in.3, bf16[4,768,256]{2,1,0:T(8,128)(2,1)} %bitcast.24, f32[768,128]{1,0:T(8,128)} %get-tuple-element.25.cosine, ...), custom_call_target="tpu_custom_call" | custom-call | tf_op jit(solution)/shard_map/pallas_call | solution.py:880
  129.5 94.5 %shard_map.177 = (bf16[4,768,256]{2,1,0:T(8,128)(2,1)}, bf16[512,393]{1,0:T(8,128)(2,1)}) custom-call(f32[2,4]{1,0:T(2,128)} %hc_in.3, f32[2,4,4]{2,1,0:T(4,128)} %hc_mix.1, f32[2,4]{1,0:T(2,128)} %hc_out.1, s32[16]{0:T(128)} %accepted.1, bf16[768,256]{1,0:T(8,128)(2,1)} %get-tuple-element.6.attended, bf16[4,768,256]{2,1,0:T(8,128)(2,1)} %bitcast.25, ...), custom_call_target="tpu_custom_call" | custom-call | tf_op jit(solution)/shard_map/pallas_call | solution.py:1465
  224.1 0.0 copy-start.1
  224.1 2.2 reshape.150
  226.2 6.0 %all-to-all-start = ((bf16[256,2,393]{2,1,0:T(2,128)(2,1)}), bf16[256,2,393]{2,1,0:T(2,128)(2,1)S(1)}, u32[]{:S(2)}, u32[]{:S(2)}) async-start(bf16[256,2,393]{2,1,0:T(2,128)(2,1)} %reshape.150), calls=%async_computation | async-start | bytes 1048576 | tf_op jit(solution)/shard_map/all_to_all | solution.py:1559
  232.3 0.0 copy-done.1
  232.3 2.4 copy.30
  234.6 11.3 %all-to-all-done = bf16[256,2,393]{2,1,0:T(2,128)(2,1)S(1)} async-done(((bf16[256,2,393]{2,1,0:T(2,128)(2,1)}), bf16[256,2,393]{2,1,0:T(2,128)(2,1)S(1)}, u32[]{:S(2)}, u32[]{:S(2)}) %all-to-all-start) | async-done | bytes 402464 | tf_op jit(solution)/shard_map/all_to_all | solution.py:1559
  245.9 0.1 copy.34
  246.1 2.1 reshape.151
  (4 shorter events, 0.0 us)
Async XLA Ops:
  0.6 6.0 %copy-start = (bf16[768,4,256]{2,1,0:T(4,128)(2,1)S(1)}, bf16[768,4,256]{2,1,0:T(4,128)(2,1)}, u32[]{:S(2)}) copy-start(bf16[768,4,256]{2,1,0:T(4,128)(2,1)} %param.17) | copy-start | bytes 4718596
  224.1 8.2 %copy-start.1 = (bf16[4,768,256]{2,1,0:T(8,128)(2,1)S(1)}, bf16[4,768,256]{2,1,0:T(8,128)(2,1)}, u32[]{:S(2)}) copy-start(bf16[4,768,256]{2,1,0:T(8,128)(2,1)} %get-tuple-element.8) | copy-start | bytes 4718596
  226.2 19.7 %all-to-all-start = ((bf16[256,2,393]{2,1,0:T(2,128)(2,1)}), bf16[256,2,393]{2,1,0:T(2,128)(2,1)S(1)}, u32[]{:S(2)}, u32[]{:S(2)}) async-start(bf16[256,2,393]{2,1,0:T(2,128)(2,1)} %reshape.150), calls=%async_computation | async-start | bytes 1048576 | tf_op jit(solution)/shard_map/all_to_all | solution.py:1559

commit v5 on v4

--- a/solution.py
+++ b/solution.py
@@ -594,6 +594,13 @@
                 total = value if total is None else total + value
             put(item, total)
 
+    def offset(order):
+        if isinstance(order, int):
+            swapped = order + order // 2 - 2 * (order // 3)
+        else:
+            swapped = order + lax.div(order, 2) - 2 * lax.div(order, 3)
+        return 2 + side - turn * swapped
+
     stat_copies = {}
     far, near = {}, {}
     for half in halves:
@@ -607,7 +614,7 @@
     for order in range(4):
         for half in halves:
             up, down = shifted(second[half], turn), shifted(second[half], -turn)
-            p1 = at(first[half], 2 - turn * order)
+            p1 = at(first[half], offset(order))
             far[half, order] = go(
                 remote(part(half, at(second[half], 2), p1), relay.at[half, p1],
                        far_send.at[half, order], far_recv.at[half, order], up))
@@ -632,26 +639,26 @@
                    stat_send.at[half, 2], stat_recv.at[half, 2], shifted(second[half], turn)))
 
     def join_copy(half, order):
-        p1 = at(first[half], 2 - turn * order)
+        p1 = at(first[half], offset(order))
         return remote(relay.at[half, p1], merged.at[half, p1],
                       join_send.at[half, order], join_recv.at[half, order],
                       shifted(second[half], turn))
 
     def far_copy(half, order):
-        p1 = at(first[half], 2 - turn * order)
+        p1 = at(first[half], offset(order))
         return remote(part(half, at(second[half], 2), p1), relay.at[half, p1],
                       far_send.at[half, order], far_recv.at[half, order],
                       shifted(second[half], turn))
 
     def near_copy(half, order):
-        p1 = at(first[half], 2 - turn * order)
+        p1 = at(first[half], offset(order))
         return remote(part(half, at(second[half], -turn), p1), single.at[half, p1],
                       near_send.at[half, order], near_recv.at[half, order],
                       shifted(second[half], -turn))
 
     def relay_step(order, carry):
         for half in halves:
-            p1 = at(first[half], 2 + side - turn * order)
+            p1 = at(first[half], offset(order))
             far_copy(half, order).wait_recv()
             lanes = pl.ds(p1 * block, block)
             target = relay.at[half, p1]
@@ -684,7 +691,7 @@
             small_s[half, p1, 1] = den[p1 * block : (p1 + 1) * block]
 
     def gather_piece(half, order):
-        p1 = at(first[half], 2 + side - turn * order)
+        p1 = at(first[half], offset(order))
         near_copy(half, order).wait_recv()
         join_copy(half, order).wait_recv()
         lanes = pl.ds(p1 * block, block)
@@ -719,8 +726,7 @@
     for half in halves:
         p1 = at(first[half], 2)
         tail(half, 0, small.at[half, p1], small_s.at[half, p1], turn)
-    lax.fori_loop(1, 2, piece_step, 0)
-    lax.fori_loop(2, 4, piece_step, 0)
+    lax.fori_loop(1, 3, piece_step, 0)
     for half in halves:
         p1 = at(first[half], -turn)
         tail(half, 1, small.at[half, p1], small_s.at[half, p1], -turn)
@@ -740,6 +746,7 @@
 
         combine(put, [target, hop.at[half, 0]], weights)
         tail(half, 2, target, small_s.at[half, p1], turn)
+    lax.fori_loop(3, 4, piece_step, 0)
     for half in halves:
         p1 = at(first[half], 0)
         for index in (1, 2):

time: 249 us -> 249 us (level)
    pallas_call x1, Pallas kernels: 94.5 us -> 97.1 us  [layer(): pl.pallas_call(functools.partial(layer_kernel, chips, chunks), out_shape=...]
where the time goes in v5:
time: 249 us
  Pallas kernels  213 us (86%)
  waiting for transfers between devices  11.3 us (5%)
  local copies, waits for them, and re-layouts  9.28 us (4%)
  other arithmetic  6.51 us (3%)
  starting transfers between devices  5.55 us (2%)
    pallas_call x1, Pallas kernels, cache_attention(): pl.pallas_call(functools.partial(cache_kernel, side, group // 2), out_sha...  116 us
    pallas_call x1, Pallas kernels, layer(): pl.pallas_call(functools.partial(layer_kernel, chips, chunks), out_shape=...  97.1 us
    all_to_all x1, waiting for transfers between devices, on_device(): lax.all_to_all(logits_local, ('req', 'head'), split_axis=0, concat_axis=2...  11.3 us
    all_to_all x1, starting transfers between devices, on_device(): lax.all_to_all(logits_local, ('req', 'head'), split_axis=0, concat_axis=2...  5.55 us
  transfers between devices with their start and end apart: 1, of which 1 were waited for; matrix products, arithmetic and copies ran while one was open for 1% of the time, Pallas kernels for 0%

profile of v5, /device:TPU:1, one launch (start us, length us, event | category | flops | bytes accessed | tf_op | source)
XLA Modules:
  0.0 248.7 jit_solution(3332691200509657346)
XLA Ops:
  0.6 0.0 copy-start
  0.7 0.8 compare_select_fusion.5
  1.5 0.2 convert_reduce_fusion.3
  1.7 0.7 select_reduce_fusion.table
  2.3 0.1 mul.93
  2.4 0.1 mul.94
  2.5 1.4 fusion.1
  4.0 0.5 fusion.3
  4.5 0.5 convert_reduce_fusion
  5.0 0.7 add_convert_fusion
  5.7 0.1 convert_element_type.81
  5.8 0.5 mul.96
  6.3 0.3 mul.97
  6.6 0.0 copy-done
  6.6 1.3 copy.33
  8.0 0.1 convert_reduce_fusion.1
  8.1 0.6 compare_select_fusion.6.last
  8.7 0.8 broadcast_multiply_fusion.mask_ref
  9.5 1.4 fusion.16
  10.9 1.2 pad_maximum_fusion
  12.1 115.8 %shard_map.176 = (bf16[768,256]{1,0:T(8,128)(2,1)}, bf16[2,2048,1024]{2,1,0:T(8,128)(2,1)}) custom-call(s32[48]{0:T(128)} %select_reduce_fusion.table, s32[256]{0:T(256)} %compare_select_fusion.6.last, f32[2,4]{1,0:T(2,128)} %hc_in.3, bf16[4,768,256]{2,1,0:T(8,128)(2,1)} %bitcast.24, f32[768,128]{1,0:T(8,128)} %get-tuple-element.25.cosine, ...), custom_call_target="tpu_custom_call" | custom-call | tf_op jit(solution)/shard_map/pallas_call | solution.py:887
  127.9 97.1 %shard_map.177 = (bf16[4,768,256]{2,1,0:T(8,128)(2,1)}, bf16[512,393]{1,0:T(8,128)(2,1)}) custom-call(f32[2,4]{1,0:T(2,128)} %hc_in.3, f32[2,4,4]{2,1,0:T(4,128)} %hc_mix.1, f32[2,4]{1,0:T(2,128)} %hc_out.1, s32[16]{0:T(128)} %accepted.1, bf16[768,256]{1,0:T(8,128)(2,1)} %get-tuple-element.6.attended, bf16[4,768,256]{2,1,0:T(8,128)(2,1)} %bitcast.25, ...), custom_call_target="tpu_custom_call" | custom-call | tf_op jit(solution)/shard_map/pallas_call | solution.py:1472
  225.0 0.0 copy-start.1
  225.0 2.2 reshape.150
  227.2 5.6 %all-to-all-start = ((bf16[256,2,393]{2,1,0:T(2,128)(2,1)}), bf16[256,2,393]{2,1,0:T(2,128)(2,1)S(1)}, u32[]{:S(2)}, u32[]{:S(2)}) async-start(bf16[256,2,393]{2,1,0:T(2,128)(2,1)} %reshape.150), calls=%async_computation | async-start | bytes 1048576 | tf_op jit(solution)/shard_map/all_to_all | solution.py:1566
  232.8 0.0 copy-done.1
  232.8 2.4 copy.30
  235.2 11.3 %all-to-all-done = bf16[256,2,393]{2,1,0:T(2,128)(2,1)S(1)} async-done(((bf16[256,2,393]{2,1,0:T(2,128)(2,1)}), bf16[256,2,393]{2,1,0:T(2,128)(2,1)S(1)}, u32[]{:S(2)}, u32[]{:S(2)}) %all-to-all-start) | async-done | bytes 402464 | tf_op jit(solution)/shard_map/all_to_all | solution.py:1566
  246.5 0.1 copy.34
  246.6 2.1 reshape.151
  (4 shorter events, 0.0 us)
Async XLA Ops:
  0.6 6.0 %copy-start = (bf16[768,4,256]{2,1,0:T(4,128)(2,1)S(1)}, bf16[768,4,256]{2,1,0:T(4,128)(2,1)}, u32[]{:S(2)}) copy-start(bf16[768,4,256]{2,1,0:T(4,128)(2,1)} %param.17) | copy-start | bytes 4718596
  225.0 7.7 %copy-start.1 = (bf16[4,768,256]{2,1,0:T(8,128)(2,1)S(1)}, bf16[4,768,256]{2,1,0:T(8,128)(2,1)}, u32[]{:S(2)}) copy-start(bf16[4,768,256]{2,1,0:T(8,128)(2,1)} %get-tuple-element.8) | copy-start | bytes 4718596
  227.2 19.2 %all-to-all-start = ((bf16[256,2,393]{2,1,0:T(2,128)(2,1)}), bf16[256,2,393]{2,1,0:T(2,128)(2,1)S(1)}, u32[]{:S(2)}, u32[]{:S(2)}) async-start(bf16[256,2,393]{2,1,0:T(2,128)(2,1)} %reshape.150), calls=%async_computation | async-start | bytes 1048576 | tf_op jit(solution)/shard_map/all_to_all | solution.py:1566

commit v6 on v5

--- a/solution.py
+++ b/solution.py
@@ -417,6 +417,15 @@
     seg_acc[slots] = jnp.zeros(seg_acc.shape[1:], seg_acc.dtype)
     tree_stat[...] = jnp.zeros(tree_stat.shape, jnp.float32)
 
+    spread_row = lax.broadcasted_iota(jnp.int32, (half_rows, rows), 0)
+    spread_col = lax.broadcasted_iota(jnp.int32, (half_rows, rows), 1)
+    spread = jnp.where(
+        jnp.logical_or(spread_col == spread_row, spread_col == spread_row + half_rows), 1.0, 0.0
+    ).astype(jnp.bfloat16)
+    key_head = lax.broadcasted_iota(jnp.int32, (rows, rows), 0) >= half_rows
+    query_head = lax.broadcasted_iota(jnp.int32, (rows, rows), 1) >= half_rows
+    same_head = key_head.astype(jnp.int32) == query_head.astype(jnp.int32)
+
     def tree_step(item, carry):
         found = lax.dot_general(
             key_ref[item],
@@ -424,7 +433,13 @@
             (((1,), (1,)), ((), ())),
             preferred_element_type=jnp.float32,
         )
-        found = jnp.where(mask_ref[item].astype(jnp.float32) > 0.0, found, NEG_FILL)
+        wide = lax.dot_general(
+            mask_ref[item], spread, (((1,), (0,)), ((), ())), preferred_element_type=jnp.float32
+        ).astype(jnp.bfloat16)
+        reached = lax.dot_general(
+            spread, wide, (((0,), (0,)), ((), ())), preferred_element_type=jnp.float32
+        )
+        found = jnp.where(jnp.logical_and(same_head, reached > 0.0), found, NEG_FILL)
         top = jnp.max(found, axis=0, keepdims=True)
         weight = jnp.exp(found - top)
         tree_acc[item] = lax.dot_general(
@@ -796,7 +811,8 @@
 def cache_attention(
     streams, hc_in, qkv, up_rows, cosine, sine, tree_mask, k_pages, v_pages, page_owner, page_fill
 ):
-    req_local, rows = tree_mask.shape[0:2]
+    req_local = tree_mask.shape[0]
+    rows = k_pages.shape[2] * tree_mask.shape[1]
     head_dim = k_pages.shape[3]
     tokens, feature = streams.shape[1:3]
     group = lax.axis_size("head")
@@ -1526,10 +1542,6 @@
     depth = (jnp.sum(reach.astype(jnp.float32), axis=1) - 1.0).astype(jnp.int32)
     positions = (cache_len[:, None] + depth).reshape(tokens_local)
     cosine, sine = turns(positions, head_dim)
-    same_head = jnp.eye(heads_local, dtype=jnp.bfloat16)
-    tree_mask = (same_head[None, :, None, :, None] * reach[:, None, :, None, :]).reshape(
-        req_local, heads_local * tree_size, heads_local * tree_size
-    )
     by_stream = jnp.transpose(streams, (1, 0, 2))
     width, kinds, inner = up_gate.shape
     up_rows = jnp.transpose(up_gate.reshape(width, kinds, inner // 128, 128), (0, 2, 1, 3)).reshape(
@@ -1542,7 +1554,7 @@
         up_rows,
         cosine,
         sine,
-        tree_mask,
+        reach,
         k_pages,
         v_pages,
         page_owner,

time: 249 us -> 250 us (level)
  no operation moved by 1% of the time
where the time goes in v6:
time: 250 us
  Pallas kernels  215 us (86%)
  waiting for transfers between devices  11.3 us (5%)
  local copies, waits for them, and re-layouts  8.24 us (3%)
  starting transfers between devices  5.81 us (2%)
  other arithmetic  5.6 us (2%)
  matrix products  3.1 us (1%)
    pallas_call x1, Pallas kernels, cache_attention(): pl.pallas_call(functools.partial(cache_kernel, side, group // 2), out_sha...  117 us
    pallas_call x1, Pallas kernels, layer(): pl.pallas_call(functools.partial(layer_kernel, chips, chunks), out_shape=...  97.4 us
    all_to_all x1, waiting for transfers between devices, on_device(): lax.all_to_all(logits_local, ('req', 'head'), split_axis=0, concat_axis=2...  11.3 us
    all_to_all x1, starting transfers between devices, on_device(): lax.all_to_all(logits_local, ('req', 'head'), split_axis=0, concat_axis=2...  5.81 us
  transfers between devices with their start and end apart: 1, of which 1 were waited for; matrix products, arithmetic and copies ran while one was open for 1% of the time, Pallas kernels for 0%

profile of v6, /device:TPU:1, one launch (start us, length us, event | category | flops | bytes accessed | tf_op | source)
XLA Modules:
  0.0 249.6 jit_solution(18051212997076121281)
XLA Ops:
  0.6 0.0 copy-start
  0.7 0.8 compare_select_fusion.5
  1.5 0.2 convert_reduce_fusion.3
  1.6 0.6 select_reduce_fusion.table
  2.3 1.4 fusion.1
  3.7 0.5 fusion.3
  4.2 1.2 convert_reduce_fusion
  5.4 0.7 add_convert_fusion
  6.1 0.1 convert_element_type.74
  6.2 0.0 copy-done
  6.2 1.4 copy.33
  7.5 0.1 convert_reduce_fusion.1
  7.6 0.5 compare_select_fusion.6.last
  8.2 1.4 fusion.16
  9.6 1.2 pad_maximum_fusion
  10.8 117.4 %shard_map.176 = (bf16[768,256]{1,0:T(8,128)(2,1)}, bf16[2,2048,1024]{2,1,0:T(8,128)(2,1)}) custom-call(s32[48]{0:T(128)} %select_reduce_fusion.table, s32[256]{0:T(256)} %compare_select_fusion.6.last, f32[2,4]{1,0:T(2,128)} %hc_in.3, bf16[4,768,256]{2,1,0:T(8,128)(2,1)} %bitcast.24, f32[768,128]{1,0:T(8,128)} %get-tuple-element.25.cosine, ...), custom_call_target="tpu_custom_call" | custom-call | tf_op jit(solution)/shard_map/pallas_call | solution.py:903
  128.2 97.4 %shard_map.177 = (bf16[4,768,256]{2,1,0:T(8,128)(2,1)}, bf16[512,393]{1,0:T(8,128)(2,1)}) custom-call(f32[2,4]{1,0:T(2,128)} %hc_in.3, f32[2,4,4]{2,1,0:T(4,128)} %hc_mix.1, f32[2,4]{1,0:T(2,128)} %hc_out.1, s32[16]{0:T(128)} %accepted.1, bf16[768,256]{1,0:T(8,128)(2,1)} %get-tuple-element.6.attended, bf16[4,768,256]{2,1,0:T(8,128)(2,1)} %bitcast.25, ...), custom_call_target="tpu_custom_call" | custom-call | tf_op jit(solution)/shard_map/pallas_call | solution.py:1488
  225.6 0.0 copy-start.1
  225.6 2.2 reshape.138
  227.8 5.8 %all-to-all-start = ((bf16[256,2,393]{2,1,0:T(2,128)(2,1)}), bf16[256,2,393]{2,1,0:T(2,128)(2,1)S(1)}, u32[]{:S(2)}, u32[]{:S(2)}) async-start(bf16[256,2,393]{2,1,0:T(2,128)(2,1)} %reshape.138), calls=%async_computation | async-start | bytes 1048576 | tf_op jit(solution)/shard_map/all_to_all | solution.py:1578
  233.6 0.0 copy-done.1
  233.6 2.4 copy.30
  236.0 11.3 %all-to-all-done = bf16[256,2,393]{2,1,0:T(2,128)(2,1)S(1)} async-done(((bf16[256,2,393]{2,1,0:T(2,128)(2,1)}), bf16[256,2,393]{2,1,0:T(2,128)(2,1)S(1)}, u32[]{:S(2)}, u32[]{:S(2)}) %all-to-all-start) | async-done | bytes 402464 | tf_op jit(solution)/shard_map/all_to_all | solution.py:1578
  247.3 0.1 copy.34
  247.5 2.1 reshape.139
  (3 shorter events, 0.0 us)
Async XLA Ops:
  0.6 5.6 %copy-start = (bf16[768,4,256]{2,1,0:T(4,128)(2,1)S(1)}, bf16[768,4,256]{2,1,0:T(4,128)(2,1)}, u32[]{:S(2)}) copy-start(bf16[768,4,256]{2,1,0:T(4,128)(2,1)} %param.17) | copy-start | bytes 4718596
  225.6 8.0 %copy-start.1 = (bf16[4,768,256]{2,1,0:T(8,128)(2,1)S(1)}, bf16[4,768,256]{2,1,0:T(8,128)(2,1)}, u32[]{:S(2)}) copy-start(bf16[4,768,256]{2,1,0:T(8,128)(2,1)} %get-tuple-element.8) | copy-start | bytes 4718596
  227.8 19.5 %all-to-all-start = ((bf16[256,2,393]{2,1,0:T(2,128)(2,1)}), bf16[256,2,393]{2,1,0:T(2,128)(2,1)S(1)}, u32[]{:S(2)}, u32[]{:S(2)}) async-start(bf16[256,2,393]{2,1,0:T(2,128)(2,1)} %reshape.138), calls=%async_computation | async-start | bytes 1048576 | tf_op jit(solution)/shard_map/all_to_all | solution.py:1578
